TPU v7x, 256 devices: a whole 4x4x8 slice. The times are simulated.
256 devices in a mesh: seq: 32 (over z_lo, x, core), cam: 4 (over y), tp: 2 (over z_hi).
Axes of the slice: x: 4, y: 4, z: 8 (z_hi: 2, z_lo: 4; z = z_hi * 4 + z_lo), core: 2. Of those that a mesh axis runs over, the one named last changes fastest.
Arguments:
- pixel_feature: bfloat16 [32768, 2048], P(('seq', 'cam'), 'tp'), may hold values from -6 to 6
- depth_score: float32 [32768, 59], P(('seq', 'cam')), may hold values from 0.05 to 5
- depth_bin: int32 [32768, 4], P(('seq', 'cam')), may hold values from 0 to 58
- cell_owner: int32 [131072, 1], P(('seq', 'cam')), may hold values from 0 to 31; in each aligned block of 1024 rows (0 to 1023, 1024 to 2047, ...) at most 64 rows name the same one
- cell_local: int32 [32768, 4], P(('seq', 'cam')), may hold values from 0 to 7
- frame_keep: int32 [64], replicated, may hold values 0 or 1
- norm_gain: float32 [2048], P('tp'), may hold values from 0.1 to 1.9
- w_query: bfloat16 [2048, 2048], P(None, ('cam', 'tp')), may hold values from -1.5 to 1.5
- w_key: bfloat16 [2048, 2048], P(None, ('cam', 'tp')), may hold values from -0.375 to 0.375
- w_value: bfloat16 [2048, 2048], P(None, ('cam', 'tp')), may hold values from -0.125 to 0.125
Outputs:
- attended: bfloat16 [16384, 2048], P('seq', ('cam', 'tp'))
Inputs may be any that keep to these rules, and one draw needn't show every extreme that they name: `cell_owner`: among the 1024 points of one index of seq and cam (aligned blocks of rows), no owner is named more than 64 times, a bound that some block reaches.
All inputs are finite; a program needn't handle non-finite values.
Results may differ from a plain program's by a relative error of at most 0.028.
The roundings to bfloat16 on the way count: a program that leaves them out, or rounds other values in their place, can miss the bound.
Values may be sent and summed in bfloat16 or wider, within the bound.
A program may use at most 64 MiB of HBM per device.

v0:
```python
import jax
import jax.numpy as jnp
from jax import lax
from jax.sharding import PartitionSpec as P

D = 2048
HD = 128
CELL_DEV = 8


epsilon = 1e-05
block_rows = 512


def attend(state, query, query_start, keys, values, key_start, frame_keep):
    frames = frame_keep.shape[0]
    frame_query = (query_start + jnp.arange(query.shape[0], dtype=jnp.int32)) % frames
    frame_key = (key_start + jnp.arange(keys.shape[0], dtype=jnp.int32)) % frames
    frame_list = jnp.arange(frames, dtype=jnp.int32)
    kept = jnp.sum(
        jnp.where(frame_key[:, None] == frame_list[None, :], frame_keep[None, :], 0), axis=1
    )
    allowed = (frame_key[None, :] <= frame_query[:, None]) & (
        (kept[None, :] > 0) | (frame_key[None, :] == frame_query[:, None])
    )
    scores = jnp.einsum("qhd,khd->hqk", query, keys, preferred_element_type=jnp.float32) * (
        1.0 / HD**0.5
    )
    accum, peak, total = state
    new_peak = jnp.maximum(peak, jnp.max(jnp.where(allowed[None], scores, -1e30), axis=2))
    factor = jnp.exp(peak - new_peak)
    expo = jnp.where(allowed[None], jnp.exp(scores - new_peak[:, :, None]), 0.0)
    mixed = jnp.einsum(
        "hqk,khd->hqd", expo.astype(jnp.bfloat16), values, preferred_element_type=jnp.float32
    )
    return (accum * factor[:, :, None] + mixed, new_peak, total * factor + jnp.sum(expo, axis=2))


def local(
    pixel_feature,
    depth_score,
    depth_bin,
    cell_owner,
    cell_local,
    frame_keep,
    norm_gain,
    w_query,
    w_key,
    w_value,
):
    pixels, half = pixel_feature.shape
    keep_count = depth_bin.shape[1]
    points = pixels * keep_count
    seq_count = lax.axis_size("seq")
    seq_index = lax.axis_index("seq")
    frames = frame_keep.shape[0]
    frames_dev = frames // seq_count
    tokens_dev = CELL_DEV * frames
    capacity = 2 * points // seq_count
    prob = depth_score / jnp.sum(depth_score, axis=1, keepdims=True)
    bins = jnp.arange(depth_score.shape[1], dtype=jnp.int32)
    picked = jnp.sum(
        jnp.where(depth_bin[:, :, None] == bins[None, None, :], prob[:, None, :], 0.0), axis=2
    )
    weight = picked.astype(jnp.bfloat16)
    point_index = jnp.arange(points, dtype=jnp.int32).reshape(pixels, keep_count)
    local_frame = point_index // (points // frames_dev)
    owner = cell_owner[:, 0].reshape(pixels, keep_count)
    owner_flat = owner.reshape(points)
    hits = (owner_flat[:, None] == jnp.arange(seq_count, dtype=jnp.int32)[None, :]).astype(
        jnp.int32
    )
    rank = jnp.sum(jnp.cumsum(hits, axis=0) * hits, axis=1) - 1
    slot = owner_flat * capacity + rank
    point_rows = jnp.repeat(pixel_feature, keep_count, axis=0)
    send_rows = jnp.zeros((seq_count * capacity, half), jnp.bfloat16).at[slot].set(point_rows)
    send_rows = send_rows.reshape(seq_count, capacity, half)
    frame_global = seq_index * frames_dev + local_frame
    describe = jnp.stack(
        [
            weight.reshape(points),
            cell_local.reshape(points).astype(jnp.bfloat16),
            frame_global.reshape(points).astype(jnp.bfloat16),
        ],
        axis=0,
    )
    send_meta = jnp.zeros((3, seq_count * capacity), jnp.bfloat16).at[:, slot].set(describe)
    send_meta = send_meta.reshape(3, seq_count, capacity).transpose(1, 0, 2)
    got_rows, got_meta = (
        lax.all_to_all(send_rows, "seq", split_axis=0, concat_axis=0, tiled=True),
        lax.all_to_all(send_meta, "seq", split_axis=0, concat_axis=0, tiled=True),
    )
    target = (
        got_meta[:, 1, :].astype(jnp.float32) * frames + got_meta[:, 2, :].astype(jnp.float32)
    ).reshape(-1)
    token_ids = jnp.arange(tokens_dev, dtype=jnp.float32)
    mixing = jnp.where(
        token_ids[:, None] == target[None, :], got_meta[:, 0, :].reshape(-1)[None, :], 0
    )
    pooled = jnp.dot(mixing, got_rows.reshape(-1, half), preferred_element_type=jnp.float32)
    bev = lax.psum(pooled, "cam")
    squares = lax.psum(jnp.sum(bev * bev, axis=1), "tp")
    normed = (bev * lax.rsqrt(squares[:, None] / D + epsilon) * norm_gain[None, :]).astype(
        jnp.bfloat16
    )
    width = w_query.shape[1]
    heads_dev = width // HD
    piece = lax.all_gather(normed, "tp", axis=1, tiled=True)
    query_sum = jnp.dot(piece, w_query, preferred_element_type=jnp.float32)
    key_sum = jnp.dot(piece, w_key, preferred_element_type=jnp.float32)
    value_sum = jnp.dot(piece, w_value, preferred_element_type=jnp.float32)
    query = query_sum.astype(jnp.bfloat16).reshape(tokens_dev, heads_dev, HD)
    keys = key_sum.astype(jnp.bfloat16).reshape(tokens_dev, heads_dev, HD)
    values = value_sum.astype(jnp.bfloat16).reshape(tokens_dev, heads_dev, HD)
    query_start = seq_index * tokens_dev
    start_state = (
        jnp.zeros((heads_dev, tokens_dev, HD), jnp.float32),
        jnp.full((heads_dev, tokens_dev), -1e30, jnp.float32),
        jnp.zeros((heads_dev, tokens_dev), jnp.float32),
    )
    piece_keys = lax.all_gather(keys, "seq", axis=0, tiled=True)
    piece_values = lax.all_gather(values, "seq", axis=0, tiled=True)
    count = piece_keys.shape[0]

    def one_block(index, inner):
        block_keys = lax.dynamic_slice_in_dim(piece_keys, index * block_rows, block_rows, 0)
        block_values = lax.dynamic_slice_in_dim(piece_values, index * block_rows, block_rows, 0)
        return attend(
            inner, query, query_start, block_keys, block_values, index * block_rows, frame_keep
        )

    accum, peak, total = lax.fori_loop(0, count // block_rows, one_block, start_state)
    result = accum / total[:, :, None]
    return result.transpose(1, 0, 2).reshape(tokens_dev, width).astype(jnp.bfloat16)


def solution(mesh):
    return jax.shard_map(
        local,
        mesh=mesh,
        in_specs=(
            P(("seq", "cam"), "tp"),
            P(("seq", "cam"), None),
            P(("seq", "cam"), None),
            P(("seq", "cam"), None),
            P(("seq", "cam"), None),
            P(),
            P("tp"),
            P(None, ("cam", "tp")),
            P(None, ("cam", "tp")),
            P(None, ("cam", "tp")),
        ),
        out_specs=P("seq", ("cam", "tp")),
        check_vma=False,
    )
```

profile of v0, /device:TPU:1, one launch (start us, length us, event | category | flops | bytes accessed | tf_op | source)
XLA Modules:
  0.0 587.0 jit_solution(16973022452448787255)
XLA Ops:
  11.1 9.0 %reduce-window.6 = s32[32,8,128]{2,1,0:T(8,128)S(1)} reduce-window(s32[32,8,128]{2,1,0:T(8,128)S(1)} %fusion.34, s32[]{:T(128)} %constant.143.clone.1), window={size=1x1x128 pad=0_0x0_0x127_0}, to_apply=%region_0.0 | reduce-window | flops 4161536 | bytes 262148 | tf_op jit(solution)/shard_map/reduce-window
  22.4 3.3 scatter_custom_fusion
  26.7 10.0 %all-to-all-start = ((bf16[32,3,64]{2,1,0:T(4,128)(2,1)}), bf16[32,3,64]{2,1,0:T(4,128)(2,1)S(1)}, u32[]{:S(2)}, u32[]{:S(2)}) async-start(bf16[32,3,64]{2,1,0:T(4,128)(2,1)} %bitcast.8), calls=%async_computation | async-start | bytes 65536 | tf_op jit(solution)/shard_map/all_to_all | solution.py:91
  38.4 2.1 reshape.333
  40.4 8.6 %scatter_custom_fusion.1 = bf16[2048,1024]{1,0:T(8,128)(2,1)} fusion(s32[1024]{0:T(1024)S(1)} %bitcast.76, bf16[1024,1024]{1,0:T(8,128)(2,1)} %reshape.333, bf16[]{:T(256)} %constant.146.clone.1), kind=kCustom, calls=%fused_computation.44 | custom fusion | bytes 4194816 | tf_op jit(solution)/shard_map/scatter | solution.py:76
  49.0 7.8 %all-to-all-start.1 = ((bf16[32,64,1024]{2,1,0:T(8,128)(2,1)}), bf16[32,64,1024]{2,1,0:T(8,128)(2,1)}, u32[]{:S(2)}, u32[]{:S(2)}) async-start(bf16[32,64,1024]{2,1,0:T(8,128)(2,1)} %bitcast.65), calls=%async_computation.1 | async-start | bytes 8388608 | tf_op jit(solution)/shard_map/all_to_all | solution.py:90
  57.2 92.7 %all-to-all-done.1 = bf16[32,64,1024]{2,1,0:T(8,128)(2,1)} async-done(((bf16[32,64,1024]{2,1,0:T(8,128)(2,1)}), bf16[32,64,1024]{2,1,0:T(8,128)(2,1)}, u32[]{:S(2)}, u32[]{:S(2)}) %all-to-all-start.1) | async-done | bytes 4194336 | tf_op jit(solution)/shard_map/all_to_all | solution.py:90
  149.9 5.9 fusion.22
  155.8 64.2 %all-reduce.2.cloned.1.call-done = f32[512,1024]{1,0:T(8,128)} async-done(((f32[512,1024]{1,0:T(8,128)}), f32[512,1024]{1,0:T(8,128)}) %all-reduce.2.cloned.1.call-update) | async-done | bytes 2097168 | tf_op jit(solution)/shard_map/psum | solution.py:101
  221.9 7.8 %psum.15 = f32[512]{0:T(512)S(1)} all-reduce(f32[512]{0:T(512)S(1)} %multiply_reduce_fusion), channel_id=1, replica_groups=mesh['seq'=32,'cam'=4,'tp'=2] {'tp'}, use_global_device_ids=true, to_apply=%region_9.10 | all-reduce | flops 512 | bytes 4096 | tf_op jit(solution)/shard_map/psum | solution.py:102
  231.2 65.9 %all-gather.4.cloned.1.call-done = bf16[512,2048]{1,0:T(8,128)(2,1)} async-done(((bf16[512,1024]{1,0:T(8,128)(2,1)}), bf16[512,2048]{1,0:T(8,128)(2,1)}) %all-gather.4.cloned.1.call-update) | async-done | bytes 2097168 | tf_op jit(solution)/shard_map/all_gather | solution.py:108
  297.2 2.5 convolution_convert_fusion
  300.6 2.0 convolution_convert_fusion.2
  303.5 2.6 convolution_convert_fusion.1
  306.3 59.7 %all-gather.8.cloned.1.call-done = bf16[16384,2,128]{2,0,1:T(8,128)(2,1)} async-done(((bf16[512,2,128]{2,0,1:T(8,128)(2,1)}), bf16[16384,2,128]{2,0,1:T(8,128)(2,1)}) %all-gather.8.cloned.1.call-update) | async-done | bytes 8388624 | tf_op jit(solution)/shard_map/all_gather | solution.py:122
  366.0 69.0 %all-gather.6.cloned.1.call-done = bf16[16384,2,128]{2,0,1:T(8,128)(2,1)} async-done(((bf16[512,2,128]{2,0,1:T(8,128)(2,1)}), bf16[16384,2,128]{2,0,1:T(8,128)(2,1)}) %all-gather.6.cloned.1.call-update) | async-done | bytes 8388624 | tf_op jit(solution)/shard_map/all_gather | solution.py:121
  435.0 144.5 %while.20 = (s32[]{:T(128)}, f32[2,512,128]{2,1,0:T(8,128)S(1)}, f32[2,512]{1,0:T(2,128)S(1)}, f32[2,512]{1,0:T(2,128)S(1)}, s32[]{:T(128)}, /*index=5*/s32[64]{...) while((s32[]{:T(128)}, f32[2,512,128]{2,1,0:T(8,128)S(1)}, ...), condition=%wide.region_14.15_spmd.clone, body=%wide.region_10.14_spmd.clone.sunk | while | flops 275760128 | bytes 9256399 | solution.py:132
  437.5 2.0 convolution_add_fusion.2
  442.0 2.0 convolution_add_fusion.2
  446.5 2.0 convolution_add_fusion.2
  451.0 2.0 convolution_add_fusion.2
  455.5 2.0 convolution_add_fusion.2
  460.1 2.0 convolution_add_fusion.2
  464.6 2.0 convolution_add_fusion.2
  469.1 2.0 convolution_add_fusion.2
  473.6 2.0 convolution_add_fusion.2
  482.7 2.0 convolution_add_fusion.2
  487.2 2.0 convolution_add_fusion.2
  491.7 2.0 convolution_add_fusion.2
  500.7 2.0 convolution_add_fusion.2
  505.2 2.0 convolution_add_fusion.2
  509.8 2.0 convolution_add_fusion.2
  (363 shorter events, 129.2 us)
Async XLA Ops:
  6.5 290.6 %copy-start = (bf16[2048,256]{1,0:T(8,128)(2,1)S(1)}, bf16[2048,256]{1,0:T(8,128)(2,1)}, u32[]{:S(2)}) copy-start(bf16[2048,256]{1,0:T(8,128)(2,1)} %param.21) | copy-start | bytes 3145732
  26.7 22.4 %all-to-all-start = ((bf16[32,3,64]{2,1,0:T(4,128)(2,1)}), bf16[32,3,64]{2,1,0:T(4,128)(2,1)S(1)}, u32[]{:S(2)}, u32[]{:S(2)}) async-start(bf16[32,3,64]{2,1,0:T(4,128)(2,1)} %bitcast.8), calls=%async_computation | async-start | bytes 65536 | tf_op jit(solution)/shard_map/all_to_all | solution.py:91
  49.0 100.9 %all-to-all-start.1 = ((bf16[32,64,1024]{2,1,0:T(8,128)(2,1)}), bf16[32,64,1024]{2,1,0:T(8,128)(2,1)}, u32[]{:S(2)}, u32[]{:S(2)}) async-start(bf16[32,64,1024]{2,1,0:T(8,128)(2,1)} %bitcast.65), calls=%async_computation.1 | async-start | bytes 8388608 | tf_op jit(solution)/shard_map/all_to_all | solution.py:90
  56.8 163.2 %all-reduce.2.cloned.1.call-start = ((), (), s32[]{:S(2)}) async-start(), calls=%async_computation.2 | async-start | bytes 4194304 | tf_op jit(solution)/shard_map/psum | solution.py:101
  155.7 74.0 %copy-start.3 = (f32[1024]{0:T(1024)S(1)}, f32[1024]{0:T(1024)}, u32[]{:S(2)}) copy-start(f32[1024]{0:T(1024)} %param.18) | copy-start | bytes 12292
  155.8 141.4 %all-gather.4.cloned.1.call-start = ((), (), s32[]{:S(2)}) async-start(), calls=%async_computation.3 | async-start | bytes 3145728 | tf_op jit(solution)/shard_map/all_gather | solution.py:108
  220.0 9.7 %copy-start.1 = (f32[512,1024]{1,0:T(8,128)S(1)}, f32[512,1024]{1,0:T(8,128)}, u32[]{:S(2)}) copy-start(f32[512,1024]{1,0:T(8,128)} %all-reduce.2.cloned.1.call-done) | copy-start | bytes 6291460
  231.0 135.0 %all-gather.8.cloned.1.call-start = ((), (), s32[]{:S(2)}) async-start(), calls=%async_computation.5 | async-start | bytes 8650752 | tf_op jit(solution)/shard_map/all_gather | solution.py:122
  297.2 3.4 copy-start.4
  300.5 134.4 %all-gather.6.cloned.1.call-start = ((), (), s32[]{:S(2)}) async-start(), calls=%async_computation.4 | async-start | bytes 8650752 | tf_op jit(solution)/shard_map/all_gather | solution.py:121
  303.5 131.5 %copy-start.2 = (s32[64]{0:T(128)S(1)}, s32[64]{0:T(128)}, u32[]{:S(2)}) copy-start(s32[64]{0:T(128)} %param.17) | copy-start | bytes 772
Sparse Core Ops, SparseCore 0:
  155.9 64.0 all-reduce.1
  231.1 66.0 all-gather.3
  300.7 65.2 all-gather.7
  367.7 67.1 all-gather.5
where the time goes:
time: 590 us; the launch traced here: 587 us
  waiting for transfers between devices  352 us (60%)
  matrix products  124 us (21%)
  other arithmetic  50.4 us (9%)
  local copies, waits for them, and re-layouts  19.9 us (3%)
  starting transfers between devices  18.1 us (3%)
  between operations  13.3 us (2%)
  blocking collectives  7.76 us (1%)
    all_to_all x1, waiting for transfers between devices, local(): lax.all_to_all(send_rows, 'seq', split_axis=0, concat_axis=0, tiled=True)  92.7 us
    all_gather x1, waiting for transfers between devices, local(): piece_keys = lax.all_gather(keys, 'seq', axis=0, tiled=True)  69 us
    all_gather x1, waiting for transfers between devices, local(): piece = lax.all_gather(normed, 'tp', axis=1, tiled=True)  65.9 us
    psum x1, waiting for transfers between devices, local(): bev = lax.psum(pooled, 'cam')  64.2 us
    dot_general x32, matrix products, attend(): jnp.einsum('hqk,khd->hqd', expo.astype(jnp.bfloat16), values, preferred_e...  62.6 us
    all_gather x1, waiting for transfers between devices, local(): piece_values = lax.all_gather(values, 'seq', axis=0, tiled=True)  59.7 us
    dot_general x32, matrix products, attend(): jnp.einsum('qhd,khd->hqk', query, keys, preferred_element_type=jnp.float32)  48.2 us
    reduce_sum x32, other arithmetic, attend(): jnp.sum(expo, axis=2)  15.9 us
  transfers between devices with their start and end apart: 6, of which 5 were waited for; matrix products, arithmetic and copies ran while one was open for 3% of the time, Pallas kernels for 0%

commit v1 on v0

v1 whole, which is shorter than its diff:
```python
import functools
import math

import jax
import jax.numpy as jnp
from jax import lax
from jax.experimental import pallas as pl
from jax.experimental.pallas import tpu as pltpu
from jax.sharding import PartitionSpec as P

MESH = pl.DeviceIdType.MESH
D = 2048
HALF = 1024
HD = 128
EPS = 1e-05
PIX = 256
CELLS = 256
TOK = 512
CH = 4
ROWS = PIX // CH
BF = jnp.bfloat16
F32 = jnp.float32


def where_am_i():
    seq = lax.axis_index("seq")
    cam = lax.axis_index("cam")
    tp = lax.axis_index("tp")
    z_lo = seq // 8
    x = lax.rem(seq // 2, 4)
    core = lax.rem(seq, 2)
    return seq, cam, tp, z_lo, x, core


def gather_project(
    x_ref, meta_ref, gain_ref, wq_hbm, wk_hbm, wv_hbm, q_ref, kv_ref,
    xg, metag, gaing, ru, rd, w_s, bev, nrm,
    xsend, xrecv, zsend, zrecv, psend, precv, fsend, msend, mrecv, gsend, grecv, lsem,
):
    seq, cam, tp, z_lo, x, core = where_am_i()
    z = tp * 4 + z_lo
    up, down = lax.rem(cam + 1, 4), lax.rem(cam + 3, 4)
    across = lax.rem(cam + 2, 4)

    def at_y(c):
        return (seq, c, tp)

    def at_z(step):
        zz = lax.rem(z + step + 8, 8)
        return (lax.rem(zz, 4) * 8 + lax.rem(seq, 8), cam, zz // 4)

    barrier = pltpu.get_barrier_semaphore()
    peers = [at_y(up), at_y(down), at_y(across), at_z(1), at_z(-1), at_z(3), at_z(-3), at_z(4)]
    for peer in peers:
        pl.semaphore_signal(barrier, inc=1, device_id=peer, device_id_type=MESH)

    loads = []
    for n, w in enumerate((wq_hbm, wk_hbm, wv_hbm)):
        loads.append(pltpu.make_async_copy(w, w_s.at[n], lsem.at[n]))
    loads.append(pltpu.make_async_copy(meta_ref, metag.at[0], lsem.at[3]))
    loads.append(pltpu.make_async_copy(gain_ref, gaing.at[0], lsem.at[4]))
    for half in range(2):
        loads.append(
            pltpu.make_async_copy(x_ref.at[half], xg.at[0, half, 0], lsem.at[5 + half])
        )
    for load in loads:
        load.start()
    pl.semaphore_wait(barrier, len(peers))

    def remote(src, dst, send, recv, device):
        copy = pltpu.make_async_remote_copy(
            src_ref=src, dst_ref=dst, send_sem=send, recv_sem=recv, device_id=device,
            device_id_type=MESH,
        )
        copy.start()
        return copy

    def piece(ref, c):
        return ref.at[pl.ds((c % 2) * ROWS, ROWS)]

    sent = []
    for c in (0, 2, 1, 3):
        target = ru if c < 2 else rd
        sent.append(
            remote(
                piece(x_ref.at[c // 2], c), target.at[c % 2], zsend.at[c], zrecv.at[c],
                at_z(1) if c < 2 else at_z(-1),
            )
        )

    def spread(source, p, c, toward):
        rel = 3 if toward == 0 else 1
        sent.append(
            remote(
                source, piece(xg.at[p, c // 2, rel], c), xsend.at[p, toward, c],
                xrecv.at[p, rel, c], at_y(up if toward == 0 else down),
            )
        )

    def arrived(p, rel, c):
        ref = piece(xg.at[p, c // 2, rel], c)
        pltpu.make_async_remote_copy(
            src_ref=ref, dst_ref=ref, send_sem=xsend.at[p, 0, c], recv_sem=xrecv.at[p, rel, c],
            device_id=at_y(up), device_id_type=MESH,
        ).wait_recv()

    def forward(p, rel, c):
        ref = piece(xg.at[p, c // 2, rel], c)
        sent.append(
            remote(
                ref, piece(xg.at[p, c // 2, 2], c), fsend.at[p, c], xrecv.at[p, 2, c],
                at_y(down if rel == 1 else up),
            )
        )

    sent.append(remote(meta_ref, metag.at[3], msend.at[0], mrecv.at[0], at_y(up)))
    sent.append(remote(meta_ref, metag.at[1], msend.at[1], mrecv.at[1], at_y(down)))
    sent.append(remote(meta_ref, metag.at[2], msend.at[2], mrecv.at[2], at_y(across)))
    sent.append(remote(gain_ref, gaing.at[1], gsend, grecv, at_z(4)))
    for n in range(4):
        spread(piece(x_ref.at[(2, 3, 0, 1)[n] // 2], n), 0, (2, 3, 0, 1)[n], 0)
        spread(piece(x_ref.at[n // 2], n), 0, n, 1)

    def relay(c):
        target = ru if c < 2 else rd
        ref = target.at[c % 2]
        pltpu.make_async_remote_copy(
            src_ref=ref, dst_ref=ref, send_sem=zsend.at[c], recv_sem=zrecv.at[c],
            device_id=at_z(1), device_id_type=MESH,
        ).wait_recv()
        sent.append(
            remote(
                ref, piece(xg.at[1, c // 2, 0], c), psend.at[c], precv.at[c],
                at_z(3) if c < 2 else at_z(-3),
            )
        )

    def partner(c):
        ref = piece(xg.at[1, c // 2, 0], c)
        pltpu.make_async_remote_copy(
            src_ref=ref, dst_ref=ref, send_sem=psend.at[c], recv_sem=precv.at[c],
            device_id=at_z(3), device_id_type=MESH,
        ).wait_recv()
        spread(ref, 1, c, 0)
        spread(ref, 1, c, 1)

    for c in (0, 2, 1, 3):
        relay(c)
    for c in (2, 3):
        arrived(0, 3, c)
        forward(0, 3, c)
        arrived(0, 1, c - 2)
        forward(0, 1, c - 2)
    for c in (0, 2, 1, 3):
        partner(c)

    for n, (rel, _) in enumerate(((3, 0), (1, 1), (2, 2))):
        pltpu.make_async_remote_copy(
            src_ref=meta_ref, dst_ref=metag.at[rel], send_sem=msend.at[n], recv_sem=mrecv.at[n],
            device_id=at_y(up), device_id_type=MESH,
        ).wait_recv()
    for load in loads:
        load.wait()

    token = lax.broadcasted_iota(jnp.int32, (CELLS, 128), 0).astype(F32)

    def mixing(half):
        high, low = [], []
        for rel in range(4):
            block = metag[rel][:, half * 128 : half * 128 + 128]
            total = jnp.zeros((CELLS, 128), F32)
            for k in range(4):
                hit = token == block[4 + k : 5 + k, :]
                total = total + jnp.where(hit, block[k : k + 1, :], 0.0)
            first = total.astype(BF)
            high.append(first)
            low.append((total - first.astype(F32)).astype(BF))
        return jnp.concatenate(high, axis=1), jnp.concatenate(low, axis=1)

    mixes = [mixing(0), mixing(1)]

    def pool(p, half):
        rows = xg[p, half].reshape(4 * 128, HALF)
        high, low = mixes[half]
        bev[p, half * CELLS : half * CELLS + CELLS, :] = jnp.dot(
            high, rows, preferred_element_type=F32
        ) + jnp.dot(low, rows, preferred_element_type=F32)

    for c in range(4):
        arrived(0, 3 if c < 2 else 1, c)
    for c in range(4):
        arrived(0, 2, c)
    pool(0, 0)
    pool(0, 1)
    for c in (2, 3):
        arrived(1, 3, c)
        forward(1, 3, c)
        arrived(1, 1, c - 2)
        forward(1, 1, c - 2)
    for c in range(4):
        arrived(1, 3 if c < 2 else 1, c)
    for c in range(4):
        arrived(1, 2, c)
    pool(1, 0)
    pool(1, 1)
    pltpu.make_async_remote_copy(
        src_ref=gain_ref, dst_ref=gaing.at[1], send_sem=gsend, recv_sem=grecv,
        device_id=at_z(4), device_id_type=MESH,
    ).wait_recv()
    step = 128
    for n in range(TOK // step):
        a = bev[0, n * step : (n + 1) * step, :]
        b = bev[1, n * step : (n + 1) * step, :]
        squares = jnp.sum(a * a + b * b, axis=1, keepdims=True)
        scale = lax.rsqrt(squares / D + EPS)
        nrm[0, n * step : (n + 1) * step, :] = (a * scale * gaing[0]).astype(BF)
        nrm[1, n * step : (n + 1) * step, :] = (b * scale * gaing[1]).astype(BF)
    own = pl.multiple_of(tp * HALF, HALF)
    other = pl.multiple_of((1 - tp) * HALF, HALF)
    for n in range(3):
        result = jnp.dot(nrm[0], w_s[n, pl.ds(own, HALF), :], preferred_element_type=F32)
        result = result + jnp.dot(
            nrm[1], w_s[n, pl.ds(other, HALF), :], preferred_element_type=F32
        )
        result = result.astype(BF)
        for h in range(2):
            part = result[:, h * HD : (h + 1) * HD]
            if n == 0:
                q_ref[h] = part
            else:
                kv_ref[h, n - 1] = part
    for copy in sent:
        copy.wait_send()


def plane_gather(
    q_ref, kv_ref, qg, kvg,
    presend, prerecv, qsend, qrecv, zsend, zrecv, xsend, xrecv, fsend, csend, crecv, lsem,
):
    seq, cam, tp, z, x, core = where_am_i()
    head = lax.rem(z, 2)

    def flip(value, bit):
        low, high = lax.rem(value, 2), value // 2
        low = 1 - low if bit & 1 else low
        high = 1 - high if bit & 2 else high
        return high * 2 + low

    def device(zz, xx, cc):
        return (zz * 8 + xx * 2 + cc, cam, tp)

    def index(zz, xx, cc):
        return zz * 8 + xx * 2 + cc

    right, left, far = lax.rem(x + 1, 4), lax.rem(x + 3, 4), lax.rem(x + 2, 4)
    z1, z2 = flip(z, 1), flip(z, 2)
    sib = 1 - core
    peers = [
        device(z1, x, core), device(z2, x, core), device(z, right, core), device(z, left, core),
        device(z, x, sib),
    ]
    barrier = pltpu.get_barrier_semaphore()
    for peer in peers:
        pl.semaphore_signal(barrier, inc=1, device_id=peer, device_id_type=MESH)
    me = index(z, x, core)
    local = [
        pltpu.make_async_copy(q_ref.at[head], qg.at[head], lsem.at[0]),
        pltpu.make_async_copy(kv_ref.at[head], kvg.at[me], lsem.at[1]),
    ]
    for copy in local:
        copy.start()
    pl.semaphore_wait(barrier, len(peers))
    sent = []

    def remote(src, dst, send, recv, dev):
        copy = pltpu.make_async_remote_copy(
            src_ref=src, dst_ref=dst, send_sem=send, recv_sem=recv, device_id=dev,
            device_id_type=MESH,
        )
        copy.start()
        sent.append(copy)

    def received(ref, send, recv):
        pltpu.make_async_remote_copy(
            src_ref=ref, dst_ref=ref, send_sem=send, recv_sem=recv,
            device_id=device(z, x, sib), device_id_type=MESH,
        ).wait_recv()

    def unit(dz, dx, cc=None):
        zz = z if dz == 0 else flip(z, dz)
        xx = (x, right, far, left)[dx]
        return index(zz, xx, core if cc is None else cc)

    remote(kv_ref.at[1 - head], kvg.at[me], presend, prerecv, device(z1, x, core))
    remote(kv_ref.at[head], kvg.at[me], zsend.at[0], zrecv.at[0], device(z2, x, core))

    def spread(dz):
        u = unit(dz, 0)
        src = kv_ref.at[head] if dz == 0 else kvg.at[u]
        for order in range(2):
            for toward in range(2):
                half = 1 - order if toward == 0 else order
                rel = 3 if toward == 0 else 1
                remote(
                    src.at[half], kvg.at[u, half], xsend.at[dz, toward, half],
                    xrecv.at[dz, rel, half], device(z, right if toward == 0 else left, core),
                )
        for half in range(2):
            remote(
                src.at[half], kvg.at[u, half], csend.at[dz, 0, half], crecv.at[dz, 0, half],
                device(z, x, sib),
            )

    def arrived(dz, rel, half):
        received(kvg.at[unit(dz, rel), half], xsend.at[dz, 0, half], xrecv.at[dz, rel, half])

    def share(dz, rel, half):
        u = unit(dz, rel)
        remote(
            kvg.at[u, half], kvg.at[u, half], csend.at[dz, rel, half], crecv.at[dz, rel, half],
            device(z, x, sib),
        )

    def forward(dz):
        for rel, half in ((3, 1), (1, 0)):
            arrived(dz, rel, half)
            u = unit(dz, rel)
            remote(
                kvg.at[u, half], kvg.at[u, half], fsend.at[dz, half], xrecv.at[dz, 2, half],
                device(z, right if rel == 3 else left, core),
            )
            share(dz, rel, half)

    spread(0)
    remote(q_ref.at[1 - head], qg.at[head], qsend, qrecv, device(z1, x, core))
    received(kvg.at[unit(1, 0)], presend, prerecv)
    remote(
        kvg.at[unit(1, 0)], kvg.at[unit(1, 0)], zsend.at[1], zrecv.at[1], device(z2, x, core)
    )
    spread(1)
    forward(0)
    received(kvg.at[unit(2, 0)], zsend.at[0], zrecv.at[0])
    spread(2)
    forward(1)
    received(kvg.at[unit(3, 0)], zsend.at[1], zrecv.at[1])
    spread(3)
    forward(2)
    for dz in range(3):
        for rel, half in ((3, 0), (1, 1), (2, 0), (2, 1)):
            arrived(dz, rel, half)
            share(dz, rel, half)
    forward(3)
    for rel, half in ((3, 0), (1, 1), (2, 0), (2, 1)):
        arrived(3, rel, half)
        share(3, rel, half)
    received(qg.at[1 - head], qsend, qrecv)
    for dz in range(4):
        for rel in range(4):
            for half in range(2):
                received(
                    kvg.at[unit(dz, rel, sib), half], csend.at[dz, rel, half],
                    crecv.at[dz, rel, half],
                )
    for copy in local:
        copy.wait()
    for copy in sent:
        copy.wait_send()


SCALE = math.log2(math.e) / math.sqrt(HD)


def attention(frame_ref, kept_ref, count_ref, keep_ref, q_ref, kv_ref, o_ref, acc, top, tot):
    def block(q, rows, g, mask_from):
        unit, off = g // 2, pl.multiple_of(lax.rem(g, 2) * CELLS, CELLS)
        keys = kv_ref[unit, 0, pl.ds(off, CELLS), :]
        values = kv_ref[unit, 1, pl.ds(off, CELLS), :]
        s = lax.dot_general(q, keys, (((1,), (1,)), ((), ())), preferred_element_type=F32)
        before = top[rows, :]
        peak = jnp.maximum(before, jnp.max(s, axis=1, keepdims=True))
        factor = jnp.exp2((before - peak) * SCALE)
        e = jnp.exp2((s - jnp.concatenate([peak, peak], axis=1)) * SCALE)
        mixed = jnp.dot(e.astype(BF), values, preferred_element_type=F32)
        top[rows, :] = peak
        tot[rows, :] = tot[rows, :] * factor + (e[:, :128] + e[:, 128:])
        acc[rows, :] = acc[rows, :] * factor + mixed

    for b in range(2):
        frame = frame_ref[b]
        top[...] = jnp.full(top.shape, -1e30, F32)
        tot[...] = jnp.zeros(tot.shape, F32)
        acc[...] = jnp.zeros(acc.shape, F32)
        lower, upper = pl.ds(0, CELLS), pl.ds(CELLS, CELLS)
        block(q_ref[b, 0:CELLS, :], lower, frame, None)
        block(q_ref[b, CELLS:TOK, :], upper, frame + 1, None)

        @pl.when(keep_ref[frame] > 0)
        def _():
            block(q_ref[b, CELLS:TOK, :], upper, frame, None)

        @pl.loop(0, count_ref[frame])
        def _(i):
            block(q_ref[b], pl.ds(0, TOK), kept_ref[i], None)

        outs = []
        for f in range(2):
            rows = slice(f * CELLS, (f + 1) * CELLS)
            total = jnp.sum(tot[rows, :], axis=1, keepdims=True)
            outs.append((acc[rows, :] / total).reshape(32, 8, HD))
        o_ref[:, b] = jnp.concatenate(outs, axis=1).astype(BF)


def to_owner(o_ref, r_ref, send, recv, lsem):
    seq, cam, tp, z, x, core = where_am_i()
    barrier = pltpu.get_barrier_semaphore()

    @pl.loop(1, 32)
    def _(d):
        peer = lax.rem(seq + d, 32)
        pl.semaphore_signal(barrier, inc=1, device_id=(peer, cam, tp), device_id_type=MESH)

    local = pltpu.make_async_copy(o_ref.at[seq], r_ref.at[seq], lsem)
    local.start()
    pl.semaphore_wait(barrier, 31)

    def push(d):
        peer = lax.rem(seq + d, 32)
        return pltpu.make_async_remote_copy(
            src_ref=o_ref.at[peer], dst_ref=r_ref.at[seq], send_sem=send.at[d],
            recv_sem=recv.at[d], device_id=(peer, cam, tp), device_id_type=MESH,
        )

    @pl.loop(1, 32)
    def _(d):
        push(d).start()

    @pl.loop(1, 32)
    def _(d):
        source = lax.rem(seq + 32 - d, 32)
        pltpu.make_async_remote_copy(
            src_ref=o_ref.at[source], dst_ref=r_ref.at[source], send_sem=send.at[d],
            recv_sem=recv.at[d], device_id=(source, cam, tp), device_id_type=MESH,
        ).wait_recv()

    @pl.loop(1, 32)
    def _(d):
        push(d).wait_send()

    local.wait()


VMEM = pl.BlockSpec(memory_space=pltpu.VMEM)
ANY = pl.BlockSpec(memory_space=pl.ANY)
SMEM = pl.BlockSpec(memory_space=pltpu.SMEM)
DMA = pltpu.SemaphoreType.DMA
LIMIT = 60 * 1024 * 1024


def call_gather(x, meta, gain, wq, wk, wv):
    return pl.pallas_call(
        gather_project,
        out_shape=(
            jax.ShapeDtypeStruct((2, TOK, HD), BF),
            jax.ShapeDtypeStruct((2, 2, TOK, HD), BF),
        ),
        in_specs=[VMEM, VMEM, VMEM, ANY, ANY, ANY],
        out_specs=(VMEM, VMEM),
        scratch_shapes=[
            pltpu.VMEM((2, 2, 4, 128, HALF), BF),
            pltpu.VMEM((4, 8, PIX), F32),
            pltpu.VMEM((2, 1, HALF), F32),
            pltpu.VMEM((2, ROWS, HALF), BF),
            pltpu.VMEM((2, ROWS, HALF), BF),
            pltpu.VMEM((3, D, 2 * HD), BF),
            pltpu.VMEM((2, TOK, HALF), F32),
            pltpu.VMEM((2, TOK, HALF), BF),
            DMA((2, 2, 4)), DMA((2, 4, 4)), DMA((4,)), DMA((4,)), DMA((4,)), DMA((4,)),
            DMA((2, 4)), DMA((3,)), DMA((3,)), DMA, DMA, DMA((7,)),
        ],
        compiler_params=pltpu.CompilerParams(
            collective_id=0, has_side_effects=True, vmem_limit_bytes=LIMIT
        ),
        name="gather_project",
    )(x, meta, gain, wq, wk, wv)


def call_plane(q, kv):
    return pl.pallas_call(
        plane_gather,
        out_shape=(
            jax.ShapeDtypeStruct((2, TOK, HD), BF),
            jax.ShapeDtypeStruct((32, 2, TOK, HD), BF),
        ),
        in_specs=[VMEM, VMEM],
        out_specs=(ANY, ANY),
        scratch_shapes=[
            DMA, DMA, DMA, DMA, DMA((2,)), DMA((2,)), DMA((4, 2, 2)), DMA((4, 4, 2)),
            DMA((4, 2)), DMA((4, 4, 2)), DMA((4, 4, 2)), DMA((2,)),
        ],
        compiler_params=pltpu.CompilerParams(
            collective_id=1, has_side_effects=True, vmem_limit_bytes=LIMIT
        ),
        name="plane_gather",
    )(q, kv)


def call_attention(frames, kept, counts, keep, qg, kvg):
    return pl.pallas_call(
        attention,
        out_shape=jax.ShapeDtypeStruct((32, 2, 16, HD), BF),
        in_specs=[SMEM, SMEM, SMEM, SMEM, VMEM, VMEM],
        out_specs=VMEM,
        scratch_shapes=[
            pltpu.VMEM((TOK, HD), F32), pltpu.VMEM((TOK, HD), F32), pltpu.VMEM((TOK, HD), F32),
        ],
        compiler_params=pltpu.CompilerParams(vmem_limit_bytes=LIMIT),
        name="attention",
    )(frames, kept, counts, keep, qg, kvg)


def call_owner(o):
    return pl.pallas_call(
        to_owner,
        out_shape=jax.ShapeDtypeStruct((32, 2, 16, HD), BF),
        in_specs=[VMEM],
        out_specs=VMEM,
        scratch_shapes=[DMA((32,)), DMA((32,)), DMA],
        compiler_params=pltpu.CompilerParams(
            collective_id=2, has_side_effects=True, vmem_limit_bytes=LIMIT
        ),
        name="to_owner",
    )(o)


def local(
    pixel_feature, depth_score, depth_bin, cell_owner, cell_local, frame_keep, norm_gain,
    w_query, w_key, w_value,
):
    seq = lax.axis_index("seq")
    prob = depth_score / jnp.sum(depth_score, axis=1, keepdims=True)
    bins = jnp.arange(depth_score.shape[1], dtype=jnp.int32)
    picked = jnp.sum(
        jnp.where(depth_bin[:, :, None] == bins[None, None, :], prob[:, None, :], 0.0), axis=2
    )
    weight = lax.reduce_precision(picked, 8, 7)
    cell = (cell_owner.reshape(PIX, 4) * 8 + cell_local).astype(F32)
    meta = jnp.concatenate([weight, cell], axis=1).T
    q, kv = call_gather(
        pixel_feature.reshape(2, 128, HALF), meta, norm_gain.reshape(1, HALF), w_query, w_key,
        w_value,
    )
    qg, kvg = call_plane(q, kv)
    keep = (frame_keep > 0).astype(jnp.int32)
    order = jnp.cumsum(keep) - keep
    frames = jnp.arange(64, dtype=jnp.int32)
    kept = jnp.sum(
        jnp.where((order[None, :] == frames[:, None]) & (keep[None, :] > 0), frames[None, :], 0),
        axis=1,
    )
    pair = (seq // 16) * 16 + lax.rem(seq, 8) + jnp.array([0, 8], jnp.int32)
    o = call_attention(pair * 2, kept, order, keep, qg, kvg)
    r = call_owner(o)
    r = r.reshape(2, 2, 8, 2, 2, 8, HD)
    out = r.transpose(5, 0, 3, 2, 4, 1, 6)
    return out.reshape(TOK, 2 * HD)


def solution(mesh):
    return jax.shard_map(
        local,
        mesh=mesh,
        in_specs=(
            P(("seq", "cam"), "tp"),
            P(("seq", "cam"), None),
            P(("seq", "cam"), None),
            P(("seq", "cam"), None),
            P(("seq", "cam"), None),
            P(),
            P("tp"),
            P(None, ("cam", "tp")),
            P(None, ("cam", "tp")),
            P(None, ("cam", "tp")),
        ),
        out_specs=P("seq", ("cam", "tp")),
        check_vma=False,
    )
```

time: 590 us -> 161 us (0.27)
  waiting for transfers between devices: 352 us -> 0 us
  Pallas kernels: 0 us -> 152 us
  matrix products: 124 us -> 0 us
  other arithmetic: 50.4 us -> 7.88 us
  starting transfers between devices: 18.1 us -> 0 us
  local copies, waits for them, and re-layouts: 19.9 us -> 2.26 us
  between operations: 13.3 us -> 0.06 us
  blocking collectives: 7.76 us -> 0 us
    all_gather x3 -> x0, waiting for transfers between devices: 195 us -> none  [the longest x1 69 us: local(): piece_keys = lax.all_gather(keys, 'seq', axis=0, tiled=True)]
    pallas_call x0 -> x4, Pallas kernels: none -> 152 us  [the longest x1 55.9 us: call_plane(): pl.pallas_call(plane_gather, out_shape=(jax.ShapeDtypeStruct((2, TOK, HD)...]
    dot_general x68 -> x0, matrix products: 124 us -> none  [the longest x32 62.6 us: attend(): jnp.einsum('hqk,khd->hqd', expo.astype(jnp.bfloat16), values, preferred_e...]
    all_to_all x2 -> x0, waiting for transfers between devices: 92.7 us -> none  [the longest x1 92.7 us: local(): lax.all_to_all(send_rows, 'seq', split_axis=0, concat_axis=0, tiled=True)]
    psum x1 -> x0, waiting for transfers between devices: 64.2 us -> none  [local(): bev = lax.psum(pooled, 'cam')]
    reduce_sum x66 -> x1, other arithmetic: 21.6 us -> 0.69 us  [local(): jnp.sum(jnp.where((order[None, :] == frames[:, None]) & (keep[None, :] >...]
    all_to_all x2 -> x0, starting transfers between devices: 17.8 us -> none  [the longest x1 10 us: local(): lax.all_to_all(send_meta, 'seq', split_axis=0, concat_axis=0, tiled=True)]
    scatter x2 -> x0, local copies, waits for them, and re-layouts: 11.9 us -> none  [the longest x1 8.6 us: local(): jnp.zeros((seq_count * capacity, half), jnp.bfloat16).at[slot]]
  transfers between devices with their start and end apart: 6 -> 0, of which waited for: 5 -> 0; matrix products, arithmetic and copies ran while one was open for 3% -> 0% of each run, Pallas kernels for 0% -> 0%
where the time goes in v1:
time: 161 us; the launch traced here: 162 us
  Pallas kernels  152 us (94%)
  other arithmetic  7.88 us (5%)
  local copies, waits for them, and re-layouts  2.26 us (1%)
    pallas_call x1, Pallas kernels, call_plane(): pl.pallas_call(plane_gather, out_shape=(jax.ShapeDtypeStruct((2, TOK, HD)...  55.9 us
    pallas_call x1, Pallas kernels, call_gather(): pl.pallas_call(gather_project, out_shape=(jax.ShapeDtypeStruct((2, TOK, H...  50.5 us
    pallas_call x1, Pallas kernels, call_owner(): pl.pallas_call(to_owner, out_shape=jax.ShapeDtypeStruct((32, 2, 16, HD),...  32.6 us
    pallas_call x1, Pallas kernels, call_attention(): pl.pallas_call(attention, out_shape=jax.ShapeDtypeStruct((32, 2, 16, HD),...  13.1 us

profile of v1, /device:TPU:1, one launch (start us, length us, event | category | flops | bytes accessed | tf_op | source)
XLA Modules:
  0.0 162.2 jit_solution(12251519717967241430)
XLA Ops:
  0.0 0.6 add_multiply_fusion.frame_ref
  0.6 0.9 reduce_sum.28
  1.4 1.2 compare_convert_fusion
  2.7 0.7 multiply_reduce_fusion
  3.4 0.1 copy.21
  3.5 0.1 reduce-window.9
  3.6 0.1 reduce
  3.7 0.7 fusion.1.count_ref
  4.3 0.0 copy-start
  4.3 0.7 select_reduce_fusion.1.kept_ref
  5.0 0.8 broadcast_divide_fusion
  5.9 0.8 select_reduce_fusion
  6.7 0.1 mul.19
  6.8 0.1 copy.22
  6.9 0.7 add_convert_fusion
  7.6 0.6 maximum_bitcast_fusion.meta_ref
  8.2 50.5 %gather_project.1 = (bf16[2,512,128]{2,1,0:T(8,128)(2,1)}, bf16[2,2,512,128]{3,2,1,0:T(8,128)(2,1)}) custom-call(bf16[2,128,1024]{2,1,0:T(8,128)(2,1)} %bitcast.16, f32[8,256]{1,0:T(8,128)} %maximum_bitcast_fusion.meta_ref, f32[1,1024]{1,0:T(1,128)} %bitcast.17, bf16[2048,256]{1,0:T(8,128)(2,1)} %wq_hbm.1, bf16[2048,256]{1,0:T(8,128)(2,1)} %wk_hbm.1, ...), custom_call_target="tpu_custom_call" | custom-call | tf_op jit(solution)/shard_map/gather_project/pallas_call | solution.py:460
  58.7 55.9 %plane_gather.1 = (bf16[2,512,128]{2,1,0:T(8,128)(2,1)}, bf16[32,2,512,128]{3,2,1,0:T(8,128)(2,1)}) custom-call(bf16[2,512,128]{2,1,0:T(8,128)(2,1)} %get-tuple-element.9.q_ref, bf16[2,2,512,128]{3,2,1,0:T(8,128)(2,1)} %get-tuple-element.10.kv_ref), custom_call_target="tpu_custom_call" | custom-call | tf_op jit(solution)/shard_map/plane_gather/pallas_call | solution.py:488
  114.6 0.0 copy-done
  114.6 13.1 %attention.1.o_ref = bf16[32,2,16,128]{3,2,1,0:T(8,128)(2,1)} custom-call(s32[2]{0:T(128)} %add_multiply_fusion.frame_ref, s32[64]{0:T(128)} %select_reduce_fusion.1.kept_ref, s32[64]{0:T(128)} %copy-done, s32[64]{0:T(128)} %get-tuple-element.13.keep_ref, bf16[2,512,128]{2,1,0:T(8,128)(2,1)} %get-tuple-element.11.q_ref, ...), custom_call_target="tpu_custom_call" | custom-call | tf_op jit(solution)/shard_map/attention/pallas_call | solution.py:508
  127.7 32.6 %to_owner.1 = bf16[32,2,16,128]{3,2,1,0:T(8,128)(2,1)} custom-call(bf16[32,2,16,128]{3,2,1,0:T(8,128)(2,1)} %attention.1.o_ref), custom_call_target="tpu_custom_call" | custom-call | tf_op jit(solution)/shard_map/to_owner/pallas_call | solution.py:522
  160.3 1.2 copy.23
  161.5 0.7 copy.26
  (1 shorter events, 0.0 us)
Async XLA Ops:
  4.3 110.3 %copy-start = (s32[64]{0:T(128)}, s32[64]{0:T(128)S(1)}, u32[]{:S(2)}) copy-start(s32[64]{0:T(128)S(1)} %fusion.1.count_ref) | copy-start | bytes 772

commit v2 on v0

v2 whole, which is shorter than its diff:
```python
import functools
import math

import jax
import jax.numpy as jnp
from jax import lax
from jax.experimental import pallas as pl
from jax.experimental.pallas import tpu as pltpu
from jax.sharding import PartitionSpec as P

MESH = pl.DeviceIdType.MESH
D = 2048
HALF = 1024
HD = 128
EPS = 1e-05
PIX = 256
CELLS = 256
TOK = 512
CH = 4
ROWS = PIX // CH
BF = jnp.bfloat16
F32 = jnp.float32


def where_am_i():
    seq = lax.axis_index("seq")
    cam = lax.axis_index("cam")
    tp = lax.axis_index("tp")
    z_lo = seq // 8
    x = lax.rem(seq // 2, 4)
    core = lax.rem(seq, 2)
    return seq, cam, tp, z_lo, x, core


SCALE = math.log2(math.e) / math.sqrt(HD)
FAR = -1e30
START = -0.5e30


def fused(
    x_ref, meta_ref, gain_ref, keep_ref, wq_hbm, wk_hbm, wv_hbm, r_ref,
    xg, metag, gaing, ru, rd, w_s, bev, nrm, mix, kvb, kvs, qb, acc, top, tot, ob,
    xsend, xrecv, zsend, zrecv, psend, precv, fsend, msend, mrecv, gsend, grecv, lsem,
    bpre_s, bpre_r, bq_s, bq_r, bz_s, bz_r, bx_s, bx_r, bf_s, bc_s, bc_r, lc, d_s, d_r, ld,
):
    seq, cam, tp, z_lo, x, core = where_am_i()
    z = tp * 4 + z_lo
    up, down = lax.rem(cam + 1, 4), lax.rem(cam + 3, 4)
    across = lax.rem(cam + 2, 4)
    head = z_lo // 2

    def at_y(c):
        return (seq, c, tp)

    def at_z(step):
        zz = lax.rem(z + step + 8, 8)
        return (lax.rem(zz, 4) * 8 + lax.rem(seq, 8), cam, zz // 4)

    def flip(zz, dz):
        low = lax.rem(lax.rem(zz, 2) + (dz + 1) // 2, 2)
        high = lax.rem(zz // 2 + dz, 2)
        return high * 2 + low

    def index(zz, xx, cc):
        return zz * 8 + xx * 2 + cc

    def plane(zz, xx, cc):
        return (index(zz, xx, cc), cam, tp)

    right, left = lax.rem(x + 1, 4), lax.rem(x + 3, 4)
    sib = 1 - core
    z3, z1 = flip(z_lo, 1), flip(z_lo, 2)

    barrier = pltpu.get_barrier_semaphore()
    peers = [at_y(up), at_y(down), at_y(across), at_z(1), at_z(-1), at_z(3), at_z(-3), at_z(4)]
    for peer in peers:
        pl.semaphore_signal(barrier, inc=1, device_id=peer, device_id_type=MESH)

    @pl.loop(1, 32)
    def _(d):
        pl.semaphore_signal(
            barrier, inc=1, device_id=(lax.rem(seq + d, 32), cam, tp), device_id_type=MESH
        )

    loads = []
    for n, w in enumerate((wq_hbm, wk_hbm, wv_hbm)):
        loads.append(pltpu.make_async_copy(w, w_s.at[n], lsem.at[n]))
    loads.append(pltpu.make_async_copy(meta_ref, metag.at[0], lsem.at[3]))
    loads.append(pltpu.make_async_copy(gain_ref, gaing.at[0], lsem.at[4]))
    for half in range(2):
        loads.append(
            pltpu.make_async_copy(x_ref.at[half], xg.at[0, half, 0], lsem.at[5 + half])
        )
    for load in loads:
        load.start()
    acc[...] = jnp.zeros(acc.shape, F32)
    tot[...] = jnp.zeros(tot.shape, F32)
    top[...] = jnp.full(top.shape, START, F32)
    pl.semaphore_wait(barrier, len(peers) + 31)

    sent = []

    def describe(src, dst, send, recv, device):
        return pltpu.make_async_remote_copy(
            src_ref=src, dst_ref=dst, send_sem=send, recv_sem=recv, device_id=device,
            device_id_type=MESH,
        )

    def remote(src, dst, send, recv, device):
        copy = describe(src, dst, send, recv, device)
        copy.start()
        sent.append(copy)

    def received(ref, send, recv):
        describe(ref, ref, send, recv, at_y(up)).wait_recv()

    def piece(ref, c):
        return ref.at[pl.ds((c % 2) * ROWS, ROWS)]

    def z_out(f):
        for e in range(2):
            c = 2 * f + e
            target = ru if e == 0 else rd
            remote(
                piece(x_ref.at[f], c), target.at[f], zsend.at[c], zrecv.at[c],
                at_z(1) if e == 0 else at_z(-1),
            )

    def relay(f):
        for e in range(2):
            c = 2 * f + e
            ref = (ru if e == 0 else rd).at[f]
            received(ref, zsend.at[c], zrecv.at[c])
            remote(
                ref, piece(xg.at[1, f, 0], c), psend.at[c], precv.at[c],
                at_z(3) if e == 0 else at_z(-3),
            )

    def spread_y(source, p, c, toward):
        rel = 3 if toward == 0 else 1
        remote(
            source, piece(xg.at[p, c // 2, rel], c), xsend.at[p, toward, c],
            xrecv.at[p, rel, c], at_y(up if toward == 0 else down),
        )

    def own_y(f):
        for e in range(2):
            for toward in range(2):
                c = 2 * f + (1 - e if toward == 0 else e)
                spread_y(piece(x_ref.at[f], c), 0, c, toward)

    def got(p, rel, c):
        received(piece(xg.at[p, c // 2, rel], c), xsend.at[p, 0, c], xrecv.at[p, rel, c])

    def forward_y(p, f):
        for rel, c in ((3, 2 * f + 1), (1, 2 * f)):
            got(p, rel, c)
            ref = piece(xg.at[p, f, rel], c)
            remote(
                ref, piece(xg.at[p, f, 2], c), fsend.at[p, c], xrecv.at[p, 2, c],
                at_y(down if rel == 1 else up),
            )

    def rest_y(p, f):
        got(p, 3, 2 * f)
        got(p, 1, 2 * f + 1)
        got(p, 2, 2 * f)
        got(p, 2, 2 * f + 1)

    def partner(f):
        for e in range(2):
            c = 2 * f + e
            received(piece(xg.at[1, f, 0], c), psend.at[c], precv.at[c])
        for e in range(2):
            for toward in range(2):
                c = 2 * f + (1 - e if toward == 0 else e)
                spread_y(piece(xg.at[1, f, 0], c), 1, c, toward)

    def build_mixing(half):
        token = lax.broadcasted_iota(jnp.int32, (CELLS, 128), 0).astype(F32)
        for rel in range(4):
            block = metag[rel][:, half * 128 : half * 128 + 128]
            total = jnp.zeros((CELLS, 128), F32)
            for k in range(4):
                hit = token == block[4 + k : 5 + k, :]
                total = total + jnp.where(hit, block[k : k + 1, :], 0.0)
            first = total.astype(BF)
            mix[half, 0, :, rel * 128 : rel * 128 + 128] = first
            mix[half, 1, :, rel * 128 : rel * 128 + 128] = (
                total - first.astype(F32)
            ).astype(BF)

    def pool(p, f):
        rows = xg[p, f].reshape(4 * 128, HALF)
        bev[p, f] = jnp.dot(mix[f, 0], rows, preferred_element_type=F32) + jnp.dot(
            mix[f, 1], rows, preferred_element_type=F32
        )

    own = pl.multiple_of(tp * HALF, HALF)
    other = pl.multiple_of((1 - tp) * HALF, HALF)
    me = seq

    def project(f):
        step = 128
        for n in range(CELLS // step):
            a = bev[0, f, n * step : (n + 1) * step, :]
            b = bev[1, f, n * step : (n + 1) * step, :]
            squares = jnp.sum(a * a + b * b, axis=1, keepdims=True)
            scale = lax.rsqrt(squares / D + EPS)
            nrm[0, n * step : (n + 1) * step, :] = (a * scale * gaing[0]).astype(BF)
            nrm[1, n * step : (n + 1) * step, :] = (b * scale * gaing[1]).astype(BF)
        for n in (1, 2, 0):
            result = jnp.dot(nrm[0], w_s[n, pl.ds(own, HALF), :], preferred_element_type=F32)
            result = result + jnp.dot(
                nrm[1], w_s[n, pl.ds(other, HALF), :], preferred_element_type=F32
            )
            result = result.astype(BF)
            for h in range(2):
                part = result[:, h * HD : (h + 1) * HD]
                mine = lax.rem(head + h, 2)
                if n == 0:
                    qb[mine * 2, f] = part
                else:
                    kvs[mine, f, n - 1] = part

    def own_copies(f):
        return [
            describe(kvs.at[1, f], kvb.at[me, f], bpre_s.at[f], bpre_r.at[f], plane(z3, x, core)),
            describe(
                kvs.at[0, f], kvb.at[me, f], bz_s.at[f, 0], bz_r.at[f, 0], plane(z1, x, core)
            ),
            describe(qb.at[2, f], qb.at[1, f], bq_s.at[f], bq_r.at[f], plane(z3, x, core)),
        ]

    def issue_own(f):
        keep_copy = pltpu.make_async_copy(kvs.at[0, f], kvb.at[me, f], lc.at[f])
        keep_copy.start()
        for copy in own_copies(f):
            copy.start()
        keep_copy.wait()

    def unit(dz, dx, cc):
        return index(flip(z_lo, dz), lax.rem(x + dx, 4), cc)

    def x_copy(n, toward, kv):
        ref = kvb.at[unit(lax.rem(n, 4), 0, core), n // 4, kv]
        return describe(
            ref, ref, bx_s.at[n, toward, kv], bx_r.at[n, 3 if toward == 0 else 1, kv],
            plane(z_lo, right if toward == 0 else left, core),
        )

    def f_copy(n, kv):
        ref = kvb.at[unit(lax.rem(n, 4), 3 if kv == 1 else 1, core), n // 4, kv]
        return describe(
            ref, ref, bf_s.at[n, kv], bx_r.at[n, 2, kv],
            plane(z_lo, right if kv == 1 else left, core),
        )

    def c_copy(n, dx):
        ref = kvb.at[unit(lax.rem(n, 4), dx, core), n // 4]
        return describe(ref, ref, bc_s.at[n, dx], bc_r.at[n, dx], plane(z_lo, x, sib))

    def z_copy(f):
        ref = kvb.at[unit(1, 0, core), f]
        return describe(ref, ref, bz_s.at[f, 1], bz_r.at[f, 1], plane(z1, x, core))

    def arrived(n, rel, kv):
        ref = kvb.at[unit(lax.rem(n, 4), rel, core), n // 4, kv]
        received(ref, bx_s.at[n, 0, kv], bx_r.at[n, rel, kv])

    def stage0(n):
        f, dz = n // 4, lax.rem(n, 4)

        @pl.when(dz == 1)
        def _():
            received(kvb.at[unit(1, 0, core), f], bpre_s.at[f], bpre_r.at[f])
            z_copy(f).start()
            received(qb.at[1, f], bq_s.at[f], bq_r.at[f])

        @pl.when(dz == 2)
        def _():
            received(kvb.at[unit(2, 0, core), f], bz_s.at[f, 0], bz_r.at[f, 0])

        @pl.when(dz == 3)
        def _():
            received(kvb.at[unit(3, 0, core), f], bz_s.at[f, 1], bz_r.at[f, 1])

        x_copy(n, 0, 1).start()
        x_copy(n, 1, 0).start()
        x_copy(n, 0, 0).start()
        x_copy(n, 1, 1).start()
        c_copy(n, 0).start()

    def stage1(n):
        arrived(n, 3, 1)
        f_copy(n, 1).start()
        arrived(n, 1, 0)
        f_copy(n, 0).start()
        arrived(n, 3, 0)
        c_copy(n, 3).start()
        arrived(n, 1, 1)
        c_copy(n, 1).start()

    def stage2(n):
        arrived(n, 2, 0)
        arrived(n, 2, 1)
        c_copy(n, 2).start()

    def block(b, fq, keys, values, biases):
        q = qb[b, fq]
        s = lax.dot_general(q, keys, (((1,), (1,)), ((), ())), preferred_element_type=F32)
        before = top[b, fq]
        peak = before
        count = len(biases)
        for n in range(count):
            part = s[:, n * CELLS : (n + 1) * CELLS]
            peak = jnp.maximum(peak, jnp.max(part, axis=1, keepdims=True) + biases[n])
        factor = jnp.exp2((before - peak) * SCALE)
        total = tot[b, fq] * factor
        pieces = []
        for n in range(count):
            shift = peak - biases[n]
            for m in range(2):
                lo = n * CELLS + m * 128
                e = jnp.exp2((s[:, lo : lo + 128] - shift) * SCALE)
                total = total + e
                pieces.append(e.astype(BF))
        mixed = jnp.dot(jnp.concatenate(pieces, axis=1), values, preferred_element_type=F32)
        top[b, fq] = peak
        tot[b, fq] = total
        acc[b, fq] = acc[b, fq] * factor + mixed

    rows_of = (seq, index(z3, x, core))

    def attend(n, dx, other_core):
        dz = lax.rem(n, 4)
        cc = lax.rem(core + other_core, 2)
        u = unit(dz, dx, cc)

        @pl.when(other_core == 1)
        def _():
            received(kvb.at[u, n // 4], bc_s.at[n, dx], bc_r.at[n, dx])

        bias0 = jnp.where(keep_ref[2 * u] > 0, 0.0, FAR)
        bias1 = jnp.where(keep_ref[2 * u + 1] > 0, 0.0, FAR)
        for b in range(2):
            same = u == rows_of[b]

            @pl.when((u <= rows_of[b]) & (n < 4))
            def _():
                block(b, 0, kvb[u, 0, 0], kvb[u, 0, 1], [jnp.where(same, 0.0, bias0)])

            @pl.when((u <= rows_of[b]) & (n >= 4))
            def _():
                keys = jnp.concatenate([kvb[u, 0, 0], kvb[u, 1, 0]], axis=0)
                values = jnp.concatenate([kvb[u, 0, 1], kvb[u, 1, 1]], axis=0)
                block(b, 1, keys, values, [bias0, jnp.where(same, 0.0, bias1)])
                block(b, 0, kvb[u, 1, 0], kvb[u, 1, 1], [jnp.where(same, FAR, bias1)])

    z_out(0)
    remote(meta_ref, metag.at[3], msend.at[0], mrecv.at[0], at_y(up))
    remote(meta_ref, metag.at[1], msend.at[1], mrecv.at[1], at_y(down))
    remote(meta_ref, metag.at[2], msend.at[2], mrecv.at[2], at_y(across))
    remote(gain_ref, gaing.at[1], gsend, grecv, at_z(4))
    own_y(0)
    relay(0)
    z_out(1)
    forward_y(0, 0)
    own_y(1)
    for n, rel in enumerate((3, 1, 2)):
        received(metag.at[rel], msend.at[n], mrecv.at[n])
    for load in loads:
        load.wait()
    relay(1)
    build_mixing(0)
    forward_y(0, 1)
    partner(0)
    build_mixing(1)
    rest_y(0, 0)
    pool(0, 0)
    forward_y(1, 0)
    rest_y(0, 1)
    pool(0, 1)
    received(gaing.at[1], gsend, grecv)
    partner(1)
    rest_y(1, 0)
    pool(1, 0)
    project(0)
    issue_own(0)
    forward_y(1, 1)

    @pl.loop(0, 11)
    def _(it):
        @pl.when(it < 8)
        def _():
            stage0(it)

        @pl.when((it >= 1) & (it < 9))
        def _():
            stage1(it - 1)

        @pl.when((it >= 2) & (it < 10))
        def _():
            stage2(it - 2)

        @pl.when(it == A_AT)
        def _():
            rest_y(1, 1)
            pool(1, 1)
            project(1)
            issue_own(1)

        @pl.loop(0, 8)
        def _(j):
            n = it - 1 - (j + 5) // 8 - (j + 1) // 8
            m = lax.rem(j, 4)
            dx = m + m // 2 - (m // 3) * 2

            @pl.when((n >= 0) & (n < 8))
            def _():
                attend(n, dx, (j + 4) // 8)

    def target(device, b):
        zz = device // 8
        row = flip(zz, b) * 8 + lax.rem(device, 8)
        return row, zz // 2

    def push(d, b):
        peer = lax.rem(seq + d, 32)
        row, h = target(seq, b)
        return describe(
            ob.at[b, peer], r_ref.at[row, h], d_s.at[b, d], d_r.at[b, d], (peer, cam, tp)
        )

    local_out = []
    for b in range(2):
        outs = []
        for f in range(2):
            total = jnp.sum(tot[b, f], axis=1, keepdims=True)
            outs.append((acc[b, f] / total).reshape(32, 8, HD))
        ob[b] = jnp.concatenate(outs, axis=1).astype(BF)

        @pl.loop(1, 32)
        def _(d):
            push(d, b).start()

        row, h = target(seq, b)
        copy = pltpu.make_async_copy(ob.at[b, seq], r_ref.at[row, h], ld.at[b])
        copy.start()
        local_out.append(copy)

    for copy in sent:
        copy.wait_send()

    @pl.loop(0, 8)
    def _(n):
        for kv in range(2):
            for toward in range(2):
                x_copy(n, toward, kv).wait_send()
            f_copy(n, kv).wait_send()
        for dx in range(4):
            c_copy(n, dx).wait_send()

    for f in range(2):
        z_copy(f).wait_send()
        for copy in own_copies(f):
            copy.wait_send()

    for b in range(2):
        @pl.loop(1, 32)
        def _(d):
            source = lax.rem(seq + 32 - d, 32)
            row, h = target(source, b)
            received(r_ref.at[row, h], d_s.at[b, d], d_r.at[b, d])

        @pl.loop(1, 32)
        def _(d):
            push(d, b).wait_send()

    for copy in local_out:
        copy.wait()


A_AT = 3
VMEM = pl.BlockSpec(memory_space=pltpu.VMEM)
ANY = pl.BlockSpec(memory_space=pl.ANY)
SMEM = pl.BlockSpec(memory_space=pltpu.SMEM)
DMA = pltpu.SemaphoreType.DMA
LIMIT = 60 * 1024 * 1024


def call_fused(x, meta, gain, keep, wq, wk, wv):
    return pl.pallas_call(
        fused,
        out_shape=jax.ShapeDtypeStruct((32, 2, 16, HD), BF),
        in_specs=[VMEM, VMEM, VMEM, SMEM, ANY, ANY, ANY],
        out_specs=VMEM,
        scratch_shapes=[
            pltpu.VMEM((2, 2, 4, 128, HALF), BF),
            pltpu.VMEM((4, 8, PIX), F32),
            pltpu.VMEM((2, 1, HALF), F32),
            pltpu.VMEM((2, ROWS, HALF), BF),
            pltpu.VMEM((2, ROWS, HALF), BF),
            pltpu.VMEM((3, D, 2 * HD), BF),
            pltpu.VMEM((2, 2, CELLS, HALF), F32),
            pltpu.VMEM((2, CELLS, HALF), BF),
            pltpu.VMEM((2, 2, CELLS, 512), BF),
            pltpu.VMEM((32, 2, 2, CELLS, HD), BF),
            pltpu.VMEM((2, 2, 2, CELLS, HD), BF),
            pltpu.VMEM((3, 2, CELLS, HD), BF),
            pltpu.VMEM((2, 2, CELLS, HD), F32),
            pltpu.VMEM((2, 2, CELLS, HD), F32),
            pltpu.VMEM((2, 2, CELLS, HD), F32),
            pltpu.VMEM((2, 32, 16, HD), BF),
            DMA((2, 2, 4)), DMA((2, 4, 4)), DMA((4,)), DMA((4,)), DMA((4,)), DMA((4,)),
            DMA((2, 4)), DMA((3,)), DMA((3,)), DMA, DMA, DMA((7,)),
            DMA((2,)), DMA((2,)), DMA((2,)), DMA((2,)), DMA((2, 2)), DMA((2, 2)),
            DMA((8, 2, 2)), DMA((8, 4, 2)), DMA((8, 2)), DMA((8, 4)), DMA((8, 4)), DMA((2,)),
            DMA((2, 32)), DMA((2, 32)), DMA((2,)),
        ],
        compiler_params=pltpu.CompilerParams(
            collective_id=0, has_side_effects=True, vmem_limit_bytes=LIMIT
        ),
        name="fused",
    )(x, meta, gain, keep, wq, wk, wv)


def local(
    pixel_feature, depth_score, depth_bin, cell_owner, cell_local, frame_keep, norm_gain,
    w_query, w_key, w_value,
):
    prob = depth_score / jnp.sum(depth_score, axis=1, keepdims=True)
    bins = jnp.arange(depth_score.shape[1], dtype=jnp.int32)
    picked = jnp.sum(
        jnp.where(depth_bin[:, :, None] == bins[None, None, :], prob[:, None, :], 0.0), axis=2
    )
    weight = lax.reduce_precision(picked, 8, 7)
    cell = (cell_owner.reshape(PIX, 4) * 8 + cell_local).astype(F32)
    meta = jnp.concatenate([weight, cell], axis=1).T
    r = call_fused(
        pixel_feature.reshape(2, 128, HALF), meta, norm_gain.reshape(1, HALF), frame_keep,
        w_query, w_key, w_value,
    )
    r = r.reshape(32, 2, 2, 8, HD)
    out = r.transpose(3, 0, 2, 1, 4)
    return out.reshape(TOK, 2 * HD)


def solution(mesh):
    return jax.shard_map(
        local,
        mesh=mesh,
        in_specs=(
            P(("seq", "cam"), "tp"),
            P(("seq", "cam"), None),
            P(("seq", "cam"), None),
            P(("seq", "cam"), None),
            P(("seq", "cam"), None),
            P(),
            P("tp"),
            P(None, ("cam", "tp")),
            P(None, ("cam", "tp")),
            P(None, ("cam", "tp")),
        ),
        out_specs=P("seq", ("cam", "tp")),
        check_vma=False,
    )
```

time: 590 us -> 131 us (0.22)
  waiting for transfers between devices: 352 us -> 0 us
  Pallas kernels: 0 us -> 126 us
  matrix products: 124 us -> 0 us
  other arithmetic: 50.4 us -> 1.68 us
  starting transfers between devices: 18.1 us -> 0 us
  local copies, waits for them, and re-layouts: 19.9 us -> 3.37 us
  between operations: 13.3 us -> 0.06 us
  blocking collectives: 7.76 us -> 0 us
    all_gather x3 -> x0, waiting for transfers between devices: 195 us -> none  [the longest x1 69 us: local(): piece_keys = lax.all_gather(keys, 'seq', axis=0, tiled=True)]
    pallas_call x0 -> x1, Pallas kernels: none -> 126 us  [call_fused(): pl.pallas_call(fused, out_shape=jax.ShapeDtypeStruct((32, 2, 16, HD), BF)...]
    dot_general x68 -> x0, matrix products: 124 us -> none  [the longest x32 62.6 us: attend(): jnp.einsum('hqk,khd->hqd', expo.astype(jnp.bfloat16), values, preferred_e...]
    all_to_all x2 -> x0, waiting for transfers between devices: 92.7 us -> none  [the longest x1 92.7 us: local(): lax.all_to_all(send_rows, 'seq', split_axis=0, concat_axis=0, tiled=True)]
    psum x1 -> x0, waiting for transfers between devices: 64.2 us -> none  [local(): bev = lax.psum(pooled, 'cam')]
    reduce_sum x66 -> x0, other arithmetic: 21.6 us -> none  [the longest x32 15.9 us: attend(): jnp.sum(expo, axis=2)]
    all_to_all x2 -> x0, starting transfers between devices: 17.8 us -> none  [the longest x1 10 us: local(): lax.all_to_all(send_meta, 'seq', split_axis=0, concat_axis=0, tiled=True)]
    scatter x2 -> x0, local copies, waits for them, and re-layouts: 11.9 us -> none  [the longest x1 8.6 us: local(): jnp.zeros((seq_count * capacity, half), jnp.bfloat16).at[slot]]
  transfers between devices with their start and end apart: 6 -> 0, of which waited for: 5 -> 0; matrix products, arithmetic and copies ran while one was open for 3% -> 0% of each run, Pallas kernels for 0% -> 0%
where the time goes in v2:
time: 131 us
  Pallas kernels  126 us (96%)
  local copies, waits for them, and re-layouts  3.37 us (3%)
  other arithmetic  1.68 us (1%)
    pallas_call x1, Pallas kernels, call_fused(): pl.pallas_call(fused, out_shape=jax.ShapeDtypeStruct((32, 2, 16, HD), BF)...  126 us

profile of v2, /device:TPU:1, one launch (start us, length us, event | category | flops | bytes accessed | tf_op | source)
XLA Modules:
  0.0 130.7 jit_solution(17728548427394223827)
XLA Ops:
  0.0 0.0 copy-start
  0.0 0.0 copy-start.3
  0.0 0.9 reduce_sum.18
  0.9 0.0 copy-done.3
  1.0 0.0 copy-done
  1.0 0.0 copy-start.1
  1.0 0.7 copy-done.1
  1.7 0.1 select_reduce_fusion
  1.8 0.1 mul.11
  1.9 0.0 copy-start.2
  1.9 0.1 copy.18
  2.0 0.6 copy-done.2
  2.6 0.6 maximum_bitcast_fusion.meta_ref
  3.2 125.6 %fused.1 = bf16[32,2,16,128]{3,2,1,0:T(8,128)(2,1)} custom-call(bf16[2,128,1024]{2,1,0:T(8,128)(2,1)} %bitcast.14, f32[8,256]{1,0:T(8,128)} %maximum_bitcast_fusion.meta_ref, f32[1,1024]{1,0:T(1,128)} %bitcast.15, s32[64]{0:T(128)} %keep_ref.1, bf16[2048,256]{1,0:T(8,128)(2,1)} %wq_hbm.1, bf16[2048,256]{1,0:T(8,128)(2,1)} %wk_hbm.1, bf16[2048,256]{1,0:T(8,128)(2,1)} %wv_hbm.1), custom_call_target="tpu_custom_call" | custom-call | tf_op jit(solution)/shard_map/fused/pallas_call | solution.py:493
  128.8 1.2 copy.19
  130.0 0.7 copy.22
  (4 shorter events, 0.0 us)
Async XLA Ops:
  0.0 1.0 copy-start
  0.0 0.9 copy-start.3
  1.0 0.7 copy-start.1
  1.9 0.7 copy-start.2

commit v3 on v2

--- a/solution.py
+++ b/solution.py
@@ -58,7 +58,7 @@
 
     def flip(zz, dz):
         low = lax.rem(lax.rem(zz, 2) + (dz + 1) // 2, 2)
-        high = lax.rem(zz // 2 + dz, 2)
+        high = lax.rem(zz // 2 + dz // 2, 2)
         return high * 2 + low
 
     def index(zz, xx, cc):
@@ -69,7 +69,7 @@
 
     right, left = lax.rem(x + 1, 4), lax.rem(x + 3, 4)
     sib = 1 - core
-    z3, z1 = flip(z_lo, 1), flip(z_lo, 2)
+    z3, z1 = flip(z_lo, 2), flip(z_lo, 1)
 
     barrier = pltpu.get_barrier_semaphore()
     peers = [at_y(up), at_y(down), at_y(across), at_z(1), at_z(-1), at_z(3), at_z(-3), at_z(4)]
@@ -214,14 +214,17 @@
             result = result + jnp.dot(
                 nrm[1], w_s[n, pl.ds(other, HALF), :], preferred_element_type=F32
             )
-            result = result.astype(BF)
             for h in range(2):
                 part = result[:, h * HD : (h + 1) * HD]
                 mine = lax.rem(head + h, 2)
                 if n == 0:
-                    qb[mine * 2, f] = part
+                    qb[mine * 2, f] = part.astype(BF)
+                elif n == 1:
+                    kvs[mine, f, 0] = part.astype(BF)
                 else:
-                    kvs[mine, f, n - 1] = part
+                    flat = part.T.astype(BF)
+                    kvs[mine, f, 1, 0:HD, :] = flat[:, 0:HD]
+                    kvs[mine, f, 1, HD : 2 * HD, :] = flat[:, HD : 2 * HD]
 
     def own_copies(f):
         return [
@@ -261,7 +264,7 @@
         return describe(ref, ref, bc_s.at[n, dx], bc_r.at[n, dx], plane(z_lo, x, sib))
 
     def z_copy(f):
-        ref = kvb.at[unit(1, 0, core), f]
+        ref = kvb.at[unit(2, 0, core), f]
         return describe(ref, ref, bz_s.at[f, 1], bz_r.at[f, 1], plane(z1, x, core))
 
     def arrived(n, rel, kv):
@@ -273,13 +276,12 @@
 
         @pl.when(dz == 1)
         def _():
-            received(kvb.at[unit(1, 0, core), f], bpre_s.at[f], bpre_r.at[f])
+            received(kvb.at[unit(1, 0, core), f], bz_s.at[f, 0], bz_r.at[f, 0])
+
+        @pl.when(dz == 2)
+        def _():
+            received(kvb.at[unit(2, 0, core), f], bpre_s.at[f], bpre_r.at[f])
             z_copy(f).start()
-            received(qb.at[1, f], bq_s.at[f], bq_r.at[f])
-
-        @pl.when(dz == 2)
-        def _():
-            received(kvb.at[unit(2, 0, core), f], bz_s.at[f, 0], bz_r.at[f, 0])
 
         @pl.when(dz == 3)
         def _():
@@ -306,29 +308,36 @@
         arrived(n, 2, 1)
         c_copy(n, 2).start()
 
-    def block(b, fq, keys, values, biases):
-        q = qb[b, fq]
-        s = lax.dot_general(q, keys, (((1,), (1,)), ((), ())), preferred_element_type=F32)
-        before = top[b, fq]
-        peak = before
-        count = len(biases)
-        for n in range(count):
-            part = s[:, n * CELLS : (n + 1) * CELLS]
-            peak = jnp.maximum(peak, jnp.max(part, axis=1, keepdims=True) + biases[n])
-        factor = jnp.exp2((before - peak) * SCALE)
-        total = tot[b, fq] * factor
-        pieces = []
-        for n in range(count):
-            shift = peak - biases[n]
-            for m in range(2):
-                lo = n * CELLS + m * 128
-                e = jnp.exp2((s[:, lo : lo + 128] - shift) * SCALE)
-                total = total + e
+    def blocks(*work):
+        scores = [
+            lax.dot_general(
+                keys, qb[b, fq], (((1,), (1,)), ((), ())), preferred_element_type=F32
+            )
+            for b, fq, keys, _, _ in work
+        ]
+        done = []
+        for s, (b, fq, _, values, biases) in zip(scores, work):
+            before = top[b, fq]
+            peak = before
+            parts = [s[n * CELLS : (n + 1) * CELLS, :] for n in range(len(biases))]
+            for part, bias in zip(parts, biases):
+                peak = jnp.maximum(peak, jnp.max(part, axis=0, keepdims=True) + bias)
+            factor = jnp.exp2((before - peak) * SCALE)
+            total = tot[b, fq] * factor
+            pieces = []
+            for part, bias in zip(parts, biases):
+                e = jnp.exp2((part - (peak - bias)) * SCALE)
+                total = total + jnp.sum(e, axis=0, keepdims=True)
                 pieces.append(e.astype(BF))
-        mixed = jnp.dot(jnp.concatenate(pieces, axis=1), values, preferred_element_type=F32)
-        top[b, fq] = peak
-        tot[b, fq] = total
-        acc[b, fq] = acc[b, fq] * factor + mixed
+            mixed = jnp.dot(values, jnp.concatenate(pieces, axis=0), preferred_element_type=F32)
+            done.append((peak, total, factor, mixed))
+        for (peak, total, factor, mixed), (b, fq, _, _, _) in zip(done, work):
+            top[b, fq] = peak
+            tot[b, fq] = total
+            acc[b, fq] = acc[b, fq] * factor + mixed
+
+    def turned(u, f):
+        return jnp.concatenate([kvb[u, f, 1, 0:HD, :], kvb[u, f, 1, HD : 2 * HD, :]], axis=1)
 
     rows_of = (seq, index(z3, x, core))
 
@@ -343,19 +352,37 @@
 
         bias0 = jnp.where(keep_ref[2 * u] > 0, 0.0, FAR)
         bias1 = jnp.where(keep_ref[2 * u + 1] > 0, 0.0, FAR)
-        for b in range(2):
-            same = u == rows_of[b]
-
-            @pl.when((u <= rows_of[b]) & (n < 4))
-            def _():
-                block(b, 0, kvb[u, 0, 0], kvb[u, 0, 1], [jnp.where(same, 0.0, bias0)])
-
-            @pl.when((u <= rows_of[b]) & (n >= 4))
-            def _():
-                keys = jnp.concatenate([kvb[u, 0, 0], kvb[u, 1, 0]], axis=0)
-                values = jnp.concatenate([kvb[u, 0, 1], kvb[u, 1, 1]], axis=0)
-                block(b, 1, keys, values, [bias0, jnp.where(same, 0.0, bias1)])
-                block(b, 0, kvb[u, 1, 0], kvb[u, 1, 1], [jnp.where(same, FAR, bias1)])
+        low, high = head, 1 - head
+        low_row = jnp.minimum(rows_of[0], rows_of[1])
+        high_row = jnp.maximum(rows_of[0], rows_of[1])
+
+        def even(b, row):
+            return (b, 0, kvb[u, 0, 0], turned(u, 0), [jnp.where(u == row, 0.0, bias0)])
+
+        def odd(b, row):
+            same = u == row
+            keys = jnp.concatenate([kvb[u, 0, 0], kvb[u, 1, 0]], axis=0)
+            values = jnp.concatenate([turned(u, 0), turned(u, 1)], axis=1)
+            return [
+                (b, 1, keys, values, [bias0, jnp.where(same, 0.0, bias1)]),
+                (b, 0, kvb[u, 1, 0], turned(u, 1), [jnp.where(same, FAR, bias1)]),
+            ]
+
+        @pl.when((u <= low_row) & (n < 4))
+        def _():
+            blocks(even(low, low_row), even(high, high_row))
+
+        @pl.when((u > low_row) & (u <= high_row) & (n < 4))
+        def _():
+            blocks(even(high, high_row))
+
+        @pl.when((u <= low_row) & (n >= 4))
+        def _():
+            blocks(*odd(low, low_row), *odd(high, high_row))
+
+        @pl.when((u > low_row) & (u <= high_row) & (n >= 4))
+        def _():
+            blocks(*odd(high, high_row))
 
     z_out(0)
     remote(meta_ref, metag.at[3], msend.at[0], mrecv.at[0], at_y(up))
@@ -388,16 +415,17 @@
     project(0)
     issue_own(0)
     forward_y(1, 1)
+    stage0(lax.rem(seq, 1))
 
     @pl.loop(0, 11)
     def _(it):
-        @pl.when(it < 8)
-        def _():
-            stage0(it)
-
         @pl.when((it >= 1) & (it < 9))
         def _():
             stage1(it - 1)
+
+        @pl.when(it < 7)
+        def _():
+            stage0(it + 1)
 
         @pl.when((it >= 2) & (it < 10))
         def _():
@@ -409,6 +437,10 @@
             pool(1, 1)
             project(1)
             issue_own(1)
+
+        @pl.when((it == 1) | (it == 5))
+        def _():
+            received(qb.at[1, it // 5], bq_s.at[it // 5], bq_r.at[it // 5])
 
         @pl.loop(0, 8)
         def _(j):
@@ -422,7 +454,7 @@
 
     def target(device, b):
         zz = device // 8
-        row = flip(zz, b) * 8 + lax.rem(device, 8)
+        row = flip(zz, 2 * b) * 8 + lax.rem(device, 8)
         return row, zz // 2
 
     def push(d, b):
@@ -436,8 +468,7 @@
     for b in range(2):
         outs = []
         for f in range(2):
-            total = jnp.sum(tot[b, f], axis=1, keepdims=True)
-            outs.append((acc[b, f] / total).reshape(32, 8, HD))
+            outs.append((acc[b, f] / tot[b, f]).T.reshape(32, 8, HD))
         ob[b] = jnp.concatenate(outs, axis=1).astype(BF)
 
         @pl.loop(1, 32)
@@ -481,7 +512,7 @@
         copy.wait()
 
 
-A_AT = 3
+A_AT = 2
 VMEM = pl.BlockSpec(memory_space=pltpu.VMEM)
 ANY = pl.BlockSpec(memory_space=pl.ANY)
 SMEM = pl.BlockSpec(memory_space=pltpu.SMEM)
@@ -508,9 +539,9 @@
             pltpu.VMEM((32, 2, 2, CELLS, HD), BF),
             pltpu.VMEM((2, 2, 2, CELLS, HD), BF),
             pltpu.VMEM((3, 2, CELLS, HD), BF),
-            pltpu.VMEM((2, 2, CELLS, HD), F32),
-            pltpu.VMEM((2, 2, CELLS, HD), F32),
-            pltpu.VMEM((2, 2, CELLS, HD), F32),
+            pltpu.VMEM((2, 2, HD, CELLS), F32),
+            pltpu.VMEM((2, 2, 1, CELLS), F32),
+            pltpu.VMEM((2, 2, 1, CELLS), F32),
             pltpu.VMEM((2, 32, 16, HD), BF),
             DMA((2, 2, 4)), DMA((2, 4, 4)), DMA((4,)), DMA((4,)), DMA((4,)), DMA((4,)),
             DMA((2, 4)), DMA((3,)), DMA((3,)), DMA, DMA, DMA((7,)),

time: 131 us -> 120 us (0.916)
  Pallas kernels: 126 us -> 115 us
    pallas_call x1, Pallas kernels: 126 us -> 115 us  [call_fused(): pl.pallas_call(fused, out_shape=jax.ShapeDtypeStruct((32, 2, 16, HD), BF)...]
where the time goes in v3:
time: 120 us
  Pallas kernels  115 us (96%)
  local copies, waits for them, and re-layouts  3.37 us (3%)
  other arithmetic  1.68 us (1%)
    pallas_call x1, Pallas kernels, call_fused(): pl.pallas_call(fused, out_shape=jax.ShapeDtypeStruct((32, 2, 16, HD), BF)...  115 us

profile of v3, /device:TPU:1, one launch (start us, length us, event | category | flops | bytes accessed | tf_op | source)
XLA Modules:
  0.0 119.7 jit_solution(8710508116253629603)
XLA Ops:
  0.0 0.0 copy-start
  0.0 0.0 copy-start.3
  0.0 0.9 reduce_sum.18
  0.9 0.0 copy-done.3
  1.0 0.0 copy-done
  1.0 0.0 copy-start.1
  1.0 0.7 copy-done.1
  1.7 0.1 select_reduce_fusion
  1.8 0.1 mul.11
  1.9 0.0 copy-start.2
  1.9 0.1 copy.18
  2.0 0.6 copy-done.2
  2.6 0.6 maximum_bitcast_fusion.meta_ref
  3.2 114.6 %fused.1 = bf16[32,2,16,128]{3,2,1,0:T(8,128)(2,1)} custom-call(bf16[2,128,1024]{2,1,0:T(8,128)(2,1)} %bitcast.14, f32[8,256]{1,0:T(8,128)} %maximum_bitcast_fusion.meta_ref, f32[1,1024]{1,0:T(1,128)} %bitcast.15, s32[64]{0:T(128)} %keep_ref.1, bf16[2048,256]{1,0:T(8,128)(2,1)} %wq_hbm.1, bf16[2048,256]{1,0:T(8,128)(2,1)} %wk_hbm.1, bf16[2048,256]{1,0:T(8,128)(2,1)} %wv_hbm.1), custom_call_target="tpu_custom_call" | custom-call | tf_op jit(solution)/shard_map/fused/pallas_call | solution.py:524
  117.8 1.2 copy.19
  118.9 0.7 copy.22
  (4 shorter events, 0.0 us)
Async XLA Ops:
  0.0 1.0 copy-start
  0.0 0.9 copy-start.3
  1.0 0.7 copy-start.1
  1.9 0.7 copy-start.2

commit v4 on v3

--- a/solution.py
+++ b/solution.py
@@ -41,7 +41,7 @@
     x_ref, meta_ref, gain_ref, keep_ref, wq_hbm, wk_hbm, wv_hbm, r_ref,
     xg, metag, gaing, ru, rd, w_s, bev, nrm, mix, kvb, kvs, qb, acc, top, tot, ob,
     xsend, xrecv, zsend, zrecv, psend, precv, fsend, msend, mrecv, gsend, grecv, lsem,
-    bpre_s, bpre_r, bq_s, bq_r, bz_s, bz_r, bx_s, bx_r, bf_s, bc_s, bc_r, lc, d_s, d_r, ld,
+    bpre_s, bpre_r, bq_s, bq_r, bz_s, bz_r, bx_s, bx_r, bf_s, bc_s, bc_r, lc, d_s, d_r,
 ):
     seq, cam, tp, z_lo, x, core = where_am_i()
     z = tp * 4 + z_lo
@@ -232,7 +232,7 @@
             describe(
                 kvs.at[0, f], kvb.at[me, f], bz_s.at[f, 0], bz_r.at[f, 0], plane(z1, x, core)
             ),
-            describe(qb.at[2, f], qb.at[1, f], bq_s.at[f], bq_r.at[f], plane(z3, x, core)),
+            describe(qb.at[2, f], qb.at[1, f], bq_s.at[f], bq_r.at[f], (31 - seq, cam, tp)),
         ]
 
     def issue_own(f):
@@ -339,7 +339,7 @@
     def turned(u, f):
         return jnp.concatenate([kvb[u, f, 1, 0:HD, :], kvb[u, f, 1, HD : 2 * HD, :]], axis=1)
 
-    rows_of = (seq, index(z3, x, core))
+    rows_of = (seq, 31 - seq)
 
     def attend(n, dx, other_core):
         dz = lax.rem(n, 4)
@@ -453,18 +453,13 @@
                 attend(n, dx, (j + 4) // 8)
 
     def target(device, b):
-        zz = device // 8
-        row = flip(zz, 2 * b) * 8 + lax.rem(device, 8)
-        return row, zz // 2
+        return (31 - device if b else device), device // 16
 
     def push(d, b):
         peer = lax.rem(seq + d, 32)
         row, h = target(seq, b)
-        return describe(
-            ob.at[b, peer], r_ref.at[row, h], d_s.at[b, d], d_r.at[b, d], (peer, cam, tp)
-        )
-
-    local_out = []
+        return describe(ob.at[b, peer], r_ref.at[row, h], d_s, d_r, (peer, cam, tp))
+
     for b in range(2):
         outs = []
         for f in range(2):
@@ -476,9 +471,7 @@
             push(d, b).start()
 
         row, h = target(seq, b)
-        copy = pltpu.make_async_copy(ob.at[b, seq], r_ref.at[row, h], ld.at[b])
-        copy.start()
-        local_out.append(copy)
+        pltpu.make_async_copy(ob.at[b, seq], r_ref.at[row, h], d_r).start()
 
     for copy in sent:
         copy.wait_send()
@@ -497,19 +490,9 @@
         for copy in own_copies(f):
             copy.wait_send()
 
-    for b in range(2):
-        @pl.loop(1, 32)
-        def _(d):
-            source = lax.rem(seq + 32 - d, 32)
-            row, h = target(source, b)
-            received(r_ref.at[row, h], d_s.at[b, d], d_r.at[b, d])
-
-        @pl.loop(1, 32)
-        def _(d):
-            push(d, b).wait_send()
-
-    for copy in local_out:
-        copy.wait()
+    gone = ob.at[:, pl.ds(0, 31)]
+    pltpu.make_async_copy(gone, gone, d_s).wait()
+    pltpu.make_async_copy(r_ref, r_ref, d_r).wait()
 
 
 A_AT = 2
@@ -547,7 +530,7 @@
             DMA((2, 4)), DMA((3,)), DMA((3,)), DMA, DMA, DMA((7,)),
             DMA((2,)), DMA((2,)), DMA((2,)), DMA((2,)), DMA((2, 2)), DMA((2, 2)),
             DMA((8, 2, 2)), DMA((8, 4, 2)), DMA((8, 2)), DMA((8, 4)), DMA((8, 4)), DMA((2,)),
-            DMA((2, 32)), DMA((2, 32)), DMA((2,)),
+            DMA, DMA,
         ],
         compiler_params=pltpu.CompilerParams(
             collective_id=0, has_side_effects=True, vmem_limit_bytes=LIMIT

time: 120 us -> 117 us (0.975)
  Pallas kernels: 115 us -> 111 us
    pallas_call x1, Pallas kernels: 115 us -> 111 us  [call_fused(): pl.pallas_call(fused, out_shape=jax.ShapeDtypeStruct((32, 2, 16, HD), BF)...]
where the time goes in v4:
time: 117 us
  Pallas kernels  111 us (95%)
  local copies, waits for them, and re-layouts  3.37 us (3%)
  other arithmetic  1.68 us (1%)
    pallas_call x1, Pallas kernels, call_fused(): pl.pallas_call(fused, out_shape=jax.ShapeDtypeStruct((32, 2, 16, HD), BF)...  111 us

profile of v4, /device:TPU:1, one launch (start us, length us, event | category | flops | bytes accessed | tf_op | source)
XLA Modules:
  0.0 116.6 jit_solution(7612631944525497838)
XLA Ops:
  0.0 0.0 copy-start
  0.0 0.0 copy-start.3
  0.0 0.9 reduce_sum.18
  0.9 0.0 copy-done.3
  1.0 0.0 copy-done
  1.0 0.0 copy-start.1
  1.0 0.7 copy-done.1
  1.7 0.1 select_reduce_fusion
  1.8 0.1 mul.11
  1.9 0.0 copy-start.2
  1.9 0.1 copy.18
  2.0 0.6 copy-done.2
  2.6 0.6 maximum_bitcast_fusion.meta_ref
  3.2 111.5 %fused.1 = bf16[32,2,16,128]{3,2,1,0:T(8,128)(2,1)} custom-call(bf16[2,128,1024]{2,1,0:T(8,128)(2,1)} %bitcast.14, f32[8,256]{1,0:T(8,128)} %maximum_bitcast_fusion.meta_ref, f32[1,1024]{1,0:T(1,128)} %bitcast.15, s32[64]{0:T(128)} %keep_ref.1, bf16[2048,256]{1,0:T(8,128)(2,1)} %wq_hbm.1, bf16[2048,256]{1,0:T(8,128)(2,1)} %wk_hbm.1, bf16[2048,256]{1,0:T(8,128)(2,1)} %wv_hbm.1), custom_call_target="tpu_custom_call" | custom-call | tf_op jit(solution)/shard_map/fused/pallas_call | solution.py:507
  114.7 1.2 copy.19
  115.9 0.7 copy.22
  (4 shorter events, 0.0 us)
Async XLA Ops:
  0.0 1.0 copy-start
  0.0 0.9 copy-start.3
  1.0 0.7 copy-start.1
  1.9 0.7 copy-start.2

commit v5 on v4

--- a/solution.py
+++ b/solution.py
@@ -341,31 +341,34 @@
 
     rows_of = (seq, 31 - seq)
 
-    def attend(n, dx, other_core):
+    def attend(n, dx):
         dz = lax.rem(n, 4)
-        cc = lax.rem(core + other_core, 2)
-        u = unit(dz, dx, cc)
-
-        @pl.when(other_core == 1)
-        def _():
-            received(kvb.at[u, n // 4], bc_s.at[n, dx], bc_r.at[n, dx])
-
-        bias0 = jnp.where(keep_ref[2 * u] > 0, 0.0, FAR)
-        bias1 = jnp.where(keep_ref[2 * u + 1] > 0, 0.0, FAR)
+        received(kvb.at[unit(dz, dx, sib), n // 4], bc_s.at[n, dx], bc_r.at[n, dx])
+        u = unit(dz, dx, 0)
+        kept = [jnp.where(keep_ref[2 * u + m] > 0, 0.0, FAR) for m in range(4)]
         low, high = head, 1 - head
         low_row = jnp.minimum(rows_of[0], rows_of[1])
         high_row = jnp.maximum(rows_of[0], rows_of[1])
 
+        def bias(m, fq, row):
+            ahead = 2 * u + m
+            mine = 2 * row + fq
+            open_key = jnp.where(ahead < mine, kept[m], FAR)
+            return jnp.where(ahead == mine, 0.0, open_key)
+
         def even(b, row):
-            return (b, 0, kvb[u, 0, 0], turned(u, 0), [jnp.where(u == row, 0.0, bias0)])
+            keys = jnp.concatenate([kvb[u, 0, 0], kvb[u + 1, 0, 0]], axis=0)
+            values = jnp.concatenate([turned(u, 0), turned(u + 1, 0)], axis=1)
+            return (b, 0, keys, values, [bias(0, 0, row), bias(2, 0, row)])
 
         def odd(b, row):
-            same = u == row
-            keys = jnp.concatenate([kvb[u, 0, 0], kvb[u, 1, 0]], axis=0)
-            values = jnp.concatenate([turned(u, 0), turned(u, 1)], axis=1)
+            some = jnp.concatenate([kvb[u, 1, 0], kvb[u + 1, 1, 0]], axis=0)
+            some_v = jnp.concatenate([turned(u, 1), turned(u + 1, 1)], axis=1)
+            keys = jnp.concatenate([kvb[u, 0, 0], kvb[u + 1, 0, 0], some], axis=0)
+            values = jnp.concatenate([turned(u, 0), turned(u + 1, 0), some_v], axis=1)
             return [
-                (b, 1, keys, values, [bias0, jnp.where(same, 0.0, bias1)]),
-                (b, 0, kvb[u, 1, 0], turned(u, 1), [jnp.where(same, FAR, bias1)]),
+                (b, 1, keys, values, [bias(m, 1, row) for m in (0, 2, 1, 3)]),
+                (b, 0, some, some_v, [bias(m, 0, row) for m in (1, 3)]),
             ]
 
         @pl.when((u <= low_row) & (n < 4))
@@ -417,7 +420,7 @@
     forward_y(1, 1)
     stage0(lax.rem(seq, 1))
 
-    @pl.loop(0, 11)
+    @pl.loop(0, 10)
     def _(it):
         @pl.when((it >= 1) & (it < 9))
         def _():
@@ -442,15 +445,14 @@
         def _():
             received(qb.at[1, it // 5], bq_s.at[it // 5], bq_r.at[it // 5])
 
-        @pl.loop(0, 8)
+        @pl.loop(0, 4)
         def _(j):
-            n = it - 1 - (j + 5) // 8 - (j + 1) // 8
-            m = lax.rem(j, 4)
-            dx = m + m // 2 - (m // 3) * 2
+            n = it - 1 - j // 3
+            dx = lax.rem(3 * j, 4) - lax.rem(j // 2, 2) + 2 * (j // 3)
 
             @pl.when((n >= 0) & (n < 8))
             def _():
-                attend(n, dx, (j + 4) // 8)
+                attend(n, dx)
 
     def target(device, b):
         return (31 - device if b else device), device // 16

time: 117 us -> 110 us (0.940)
  Pallas kernels: 111 us -> 105 us
    pallas_call x1, Pallas kernels: 111 us -> 105 us  [call_fused(): pl.pallas_call(fused, out_shape=jax.ShapeDtypeStruct((32, 2, 16, HD), BF)...]
where the time goes in v5:
time: 110 us
  Pallas kernels  105 us (95%)
  local copies, waits for them, and re-layouts  3.37 us (3%)
  other arithmetic  1.68 us (2%)
    pallas_call x1, Pallas kernels, call_fused(): pl.pallas_call(fused, out_shape=jax.ShapeDtypeStruct((32, 2, 16, HD), BF)...  105 us

profile of v5, /device:TPU:1, one launch (start us, length us, event | category | flops | bytes accessed | tf_op | source)
XLA Modules:
  0.0 110.0 jit_solution(12852516625702148508)
XLA Ops:
  0.0 0.0 copy-start
  0.0 0.0 copy-start.3
  0.0 0.9 reduce_sum.18
  0.9 0.0 copy-done.3
  1.0 0.0 copy-done
  1.0 0.0 copy-start.1
  1.0 0.7 copy-done.1
  1.7 0.1 select_reduce_fusion
  1.8 0.1 mul.11
  1.9 0.0 copy-start.2
  1.9 0.1 copy.18
  2.0 0.6 copy-done.2
  2.6 0.6 maximum_bitcast_fusion.meta_ref
  3.2 104.9 %fused.1 = bf16[32,2,16,128]{3,2,1,0:T(8,128)(2,1)} custom-call(bf16[2,128,1024]{2,1,0:T(8,128)(2,1)} %bitcast.14, f32[8,256]{1,0:T(8,128)} %maximum_bitcast_fusion.meta_ref, f32[1,1024]{1,0:T(1,128)} %bitcast.15, s32[64]{0:T(128)} %keep_ref.1, bf16[2048,256]{1,0:T(8,128)(2,1)} %wq_hbm.1, bf16[2048,256]{1,0:T(8,128)(2,1)} %wk_hbm.1, bf16[2048,256]{1,0:T(8,128)(2,1)} %wv_hbm.1), custom_call_target="tpu_custom_call" | custom-call | tf_op jit(solution)/shard_map/fused/pallas_call | solution.py:509
  108.1 1.2 %copy.19 = bf16[8,32,2,2,128]{4,3,2,1,0:T(2,128)(2,1)S(1)} copy(bf16[8,32,2,2,128]{4,0,2,3,1:T(8,128)(2,1)} %bitcast.12) | data formatting | bytes 524288 | tf_op jit(solution)/shard_map/transpose | solution.py:561
  109.3 0.7 copy.22
  (4 shorter events, 0.0 us)
Async XLA Ops:
  0.0 1.0 copy-start
  0.0 0.9 copy-start.3
  1.0 0.7 copy-start.1
  1.9 0.7 copy-start.2

commit v6 on v5

--- a/solution.py
+++ b/solution.py
@@ -209,22 +209,23 @@
             scale = lax.rsqrt(squares / D + EPS)
             nrm[0, n * step : (n + 1) * step, :] = (a * scale * gaing[0]).astype(BF)
             nrm[1, n * step : (n + 1) * step, :] = (b * scale * gaing[1]).astype(BF)
-        for n in (1, 2, 0):
-            result = jnp.dot(nrm[0], w_s[n, pl.ds(own, HALF), :], preferred_element_type=F32)
-            result = result + jnp.dot(
-                nrm[1], w_s[n, pl.ds(other, HALF), :], preferred_element_type=F32
-            )
-            for h in range(2):
-                part = result[:, h * HD : (h + 1) * HD]
-                mine = lax.rem(head + h, 2)
-                if n == 0:
-                    qb[mine * 2, f] = part.astype(BF)
-                elif n == 1:
-                    kvs[mine, f, 0] = part.astype(BF)
-                else:
-                    flat = part.T.astype(BF)
-                    kvs[mine, f, 1, 0:HD, :] = flat[:, 0:HD]
-                    kvs[mine, f, 1, HD : 2 * HD, :] = flat[:, HD : 2 * HD]
+
+    def multiply(f, n):
+        result = jnp.dot(nrm[0], w_s[n, pl.ds(own, HALF), :], preferred_element_type=F32)
+        result = result + jnp.dot(
+            nrm[1], w_s[n, pl.ds(other, HALF), :], preferred_element_type=F32
+        )
+        for h in range(2):
+            part = result[:, h * HD : (h + 1) * HD]
+            mine = lax.rem(head + h, 2)
+            if n == 0:
+                qb[mine * 2, f] = part.astype(BF)
+            elif n == 1:
+                kvs[mine, f, 0] = part.astype(BF)
+            else:
+                flat = part.T.astype(BF)
+                kvs[mine, f, 1, 0:HD, :] = flat[:, 0:HD]
+                kvs[mine, f, 1, HD : 2 * HD, :] = flat[:, HD : 2 * HD]
 
     def own_copies(f):
         return [
@@ -236,11 +237,18 @@
         ]
 
     def issue_own(f):
+        multiply(f, 1)
+        multiply(f, 2)
         keep_copy = pltpu.make_async_copy(kvs.at[0, f], kvb.at[me, f], lc.at[f])
         keep_copy.start()
-        for copy in own_copies(f):
-            copy.start()
+        copies = own_copies(f)
+        copies[0].start()
+        copies[1].start()
         keep_copy.wait()
+        if f == 0:
+            stage0(lax.rem(seq, 1))
+        multiply(f, 0)
+        copies[2].start()
 
     def unit(dz, dx, cc):
         return index(flip(z_lo, dz), lax.rem(x + dx, 4), cc)
@@ -418,7 +426,6 @@
     project(0)
     issue_own(0)
     forward_y(1, 1)
-    stage0(lax.rem(seq, 1))
 
     @pl.loop(0, 10)
     def _(it):
@@ -509,7 +516,7 @@
     return pl.pallas_call(
         fused,
         out_shape=jax.ShapeDtypeStruct((32, 2, 16, HD), BF),
-        in_specs=[VMEM, VMEM, VMEM, SMEM, ANY, ANY, ANY],
+        in_specs=[ANY, VMEM, VMEM, SMEM, ANY, ANY, ANY],
         out_specs=VMEM,
         scratch_shapes=[
             pltpu.VMEM((2, 2, 4, 128, HALF), BF),

time: 110 us -> 110 us (level)
  no operation moved by 1% of the time
where the time goes in v6:
time: 110 us; the launch traced here: 109 us
  Pallas kernels  104 us (95%)
  local copies, waits for them, and re-layouts  3.37 us (3%)
  other arithmetic  1.68 us (2%)
    pallas_call x1, Pallas kernels, call_fused(): pl.pallas_call(fused, out_shape=jax.ShapeDtypeStruct((32, 2, 16, HD), BF)...  104 us

profile of v6, /device:TPU:1, one launch (start us, length us, event | category | flops | bytes accessed | tf_op | source)
XLA Modules:
  0.0 109.3 jit_solution(16616361793557849789)
XLA Ops:
  0.0 0.0 copy-start
  0.0 0.0 copy-start.3
  0.0 0.9 reduce_sum.18
  0.9 0.0 copy-done.3
  1.0 0.0 copy-done
  1.0 0.0 copy-start.1
  1.0 0.7 copy-done.1
  1.7 0.1 select_reduce_fusion
  1.8 0.1 mul.11
  1.9 0.0 copy-start.2
  1.9 0.1 copy.18
  2.0 0.6 copy-done.2
  2.6 0.6 maximum_bitcast_fusion.meta_ref
  3.2 104.2 %fused.1 = bf16[32,2,16,128]{3,2,1,0:T(8,128)(2,1)} custom-call(bf16[2,128,1024]{2,1,0:T(8,128)(2,1)} %bitcast.14, f32[8,256]{1,0:T(8,128)} %maximum_bitcast_fusion.meta_ref, f32[1,1024]{1,0:T(1,128)} %bitcast.15, s32[64]{0:T(128)} %keep_ref.1, bf16[2048,256]{1,0:T(8,128)(2,1)} %wq_hbm.1, bf16[2048,256]{1,0:T(8,128)(2,1)} %wk_hbm.1, bf16[2048,256]{1,0:T(8,128)(2,1)} %wv_hbm.1), custom_call_target="tpu_custom_call" | custom-call | tf_op jit(solution)/shard_map/fused/pallas_call | solution.py:516
  107.4 1.2 %copy.19 = bf16[8,32,2,2,128]{4,3,2,1,0:T(2,128)(2,1)S(1)} copy(bf16[8,32,2,2,128]{4,0,2,3,1:T(8,128)(2,1)} %bitcast.12) | data formatting | bytes 524288 | tf_op jit(solution)/shard_map/transpose | solution.py:568
  108.6 0.7 copy.22
  (4 shorter events, 0.0 us)
Async XLA Ops:
  0.0 1.0 copy-start
  0.0 0.9 copy-start.3
  1.0 0.7 copy-start.1
  1.9 0.7 copy-start.2

commit v7 on v6

--- a/solution.py
+++ b/solution.py
@@ -433,13 +433,13 @@
         def _():
             stage1(it - 1)
 
+        @pl.when((it >= 2) & (it < 10))
+        def _():
+            stage2(it - 2)
+
         @pl.when(it < 7)
         def _():
             stage0(it + 1)
-
-        @pl.when((it >= 2) & (it < 10))
-        def _():
-            stage2(it - 2)
 
         @pl.when(it == A_AT)
         def _():

time: 110 us -> 110 us (level)
  no operation moved by 1% of the time
where the time goes in v7:
time: 110 us; the launch traced here: 109 us
  Pallas kernels  104 us (95%)
  local copies, waits for them, and re-layouts  3.37 us (3%)
  other arithmetic  1.68 us (2%)
    pallas_call x1, Pallas kernels, call_fused(): pl.pallas_call(fused, out_shape=jax.ShapeDtypeStruct((32, 2, 16, HD), BF)...  104 us

profile of v7, /device:TPU:1, one launch (start us, length us, event | category | flops | bytes accessed | tf_op | source)
XLA Modules:
  0.0 109.3 jit_solution(6002955096419537986)
XLA Ops:
  0.0 0.0 copy-start
  0.0 0.0 copy-start.3
  0.0 0.9 reduce_sum.18
  0.9 0.0 copy-done.3
  1.0 0.0 copy-done
  1.0 0.0 copy-start.1
  1.0 0.7 copy-done.1
  1.7 0.1 select_reduce_fusion
  1.8 0.1 mul.11
  1.9 0.0 copy-start.2
  1.9 0.1 copy.18
  2.0 0.6 copy-done.2
  2.6 0.6 maximum_bitcast_fusion.meta_ref
  3.2 104.2 %fused.1 = bf16[32,2,16,128]{3,2,1,0:T(8,128)(2,1)} custom-call(bf16[2,128,1024]{2,1,0:T(8,128)(2,1)} %bitcast.14, f32[8,256]{1,0:T(8,128)} %maximum_bitcast_fusion.meta_ref, f32[1,1024]{1,0:T(1,128)} %bitcast.15, s32[64]{0:T(128)} %keep_ref.1, bf16[2048,256]{1,0:T(8,128)(2,1)} %wq_hbm.1, bf16[2048,256]{1,0:T(8,128)(2,1)} %wk_hbm.1, bf16[2048,256]{1,0:T(8,128)(2,1)} %wv_hbm.1), custom_call_target="tpu_custom_call" | custom-call | tf_op jit(solution)/shard_map/fused/pallas_call | solution.py:516
  107.4 1.2 %copy.19 = bf16[8,32,2,2,128]{4,3,2,1,0:T(2,128)(2,1)S(1)} copy(bf16[8,32,2,2,128]{4,0,2,3,1:T(8,128)(2,1)} %bitcast.12) | data formatting | bytes 524288 | tf_op jit(solution)/shard_map/transpose | solution.py:568
  108.6 0.7 copy.22
  (4 shorter events, 0.0 us)
Async XLA Ops:
  0.0 1.0 copy-start
  0.0 0.9 copy-start.3
  1.0 0.7 copy-start.1
  1.9 0.7 copy-start.2
